TPU v7x, 512 devices: a whole 4x8x8 slice. The times are simulated.
512 devices in a mesh: gx: 4 (over x), gy: 4 (over z_lo, core), gz: 32 (over z_hi, y).
Axes of the slice: x: 4, y: 8, z: 8 (z_hi: 4, z_lo: 2; z = z_hi * 2 + z_lo), core: 2. Of those that a mesh axis runs over, the one named last changes fastest.
Arguments:
- in_first: bfloat16 [262144, 1024], P(('gx', 'gy', 'gz')), may hold values from -98 to 98
- cot_first: bfloat16 [262144, 256], P(('gx', 'gy', 'gz')), may hold values from -0.05859375 to 0.05859375
- in_third: bfloat16 [262144, 256], P(('gx', 'gy', 'gz')), may hold values from -98 to 98
- cot_third: bfloat16 [262144, 1024], P(('gx', 'gy', 'gz')), may hold values from -0.05859375 to 0.05859375
- mean_old: float32 [524288], P(('gx', 'gy', 'gz')), may hold values from -6 to 6
- prec_old: float32 [524288], P(('gx', 'gy', 'gz')), may hold values from 0.5 to 4
- mom_old: float32 [524288], P(('gx', 'gy', 'gz')), may hold values from -4 to 4
- noise: bfloat16 [512, 524288], P(('gx', 'gy', 'gz')), may hold values from -6 to 6
Outputs:
- mean_new: float32 [524288], P(('gx', 'gy', 'gz'))
- prec_new: float32 [524288], P(('gx', 'gy', 'gz'))
- mom_new: float32 [524288], P(('gx', 'gy', 'gz'))
- samples: bfloat16 [512, 524288], P(('gx', 'gy', 'gz'))
All inputs are finite; a program needn't handle non-finite values.
Results may differ from a plain program's by a relative error of at most 0.0016.
Values sent between devices are 32-bit elements; how exact they have to be, the bound alone decides.
No kernel may reach another device: no remote copies, remote signals or barrier semaphores. Data moves between devices by JAX's collectives and lax.ppermute only.
A program may use at most 64 MiB of HBM per device.

v0:
```python
import jax
import jax.numpy as jnp
from jax import lax
from jax.sharding import PartitionSpec as P


def side_by_side(arrays, axis, dim, along):
    both = jnp.concatenate(arrays, axis=along)
    filled, at, outs = (lax.psum_scatter(both, axis, scatter_dimension=dim, tiled=True), 0, [])
    for a in arrays:
        outs.append(lax.slice_in_dim(filled, at, at + a.shape[along], axis=along))
        at += a.shape[along]
    return tuple(outs)


def split_up(x, dim, length):
    shape = x.shape
    pieces = x.reshape(*shape[:dim], length, shape[dim] // length, *shape[dim + 1 :])
    return jnp.moveaxis(pieces, dim, 0)


def summed_on_arrival(x, axis, dim):
    pieces = split_up(x, dim, lax.axis_size(axis))
    arrived = lax.all_to_all(pieces, axis, split_axis=0, concat_axis=0, tiled=True)
    return arrived.sum(axis=0)


def side_by_side_2(arrays, axis, dim, along):
    both = jnp.concatenate(arrays, axis=along)
    filled, at, outs = (summed_on_arrival(both, axis, dim), 0, [])
    for a in arrays:
        outs.append(lax.slice_in_dim(filled, at, at + a.shape[along], axis=along))
        at += a.shape[along]
    return tuple(outs)


def in_order(pieces, dim):
    shape = list(pieces.shape[1:])
    shape[dim] *= pieces.shape[0]
    return jnp.moveaxis(pieces, 0, dim).reshape(shape)


def from_everyone(x, axis):
    length = lax.axis_size(axis)
    return lax.all_to_all(jnp.broadcast_to(x[None], (length, *x.shape)), axis, 0, 0, tiled=True)


def gathered_copies(x, axis, dim):
    return in_order(from_everyone(x, axis), dim)


def squared(values):
    wide = values.astype(jnp.float32)
    return (wide * wide).astype(jnp.bfloat16)


def contract_rows(left, right):
    return lax.dot_general(
        left, right, (((0,), (0,)), ((), ())), preferred_element_type=jnp.float32
    )


def on_device(in_first, cot_first, in_third, cot_third, mean_old, prec_old, mom_old, noise):
    grad_first = contract_rows(in_first, cot_first)
    grad_third = contract_rows(in_third, cot_third)
    curv_first = contract_rows(squared(in_first), squared(cot_first))
    curv_third = contract_rows(squared(in_third), squared(cot_third))
    grad_flat = jnp.concatenate([grad_first.reshape(-1), grad_third.reshape(-1)])
    curv_flat = jnp.concatenate([curv_first.reshape(-1), curv_third.reshape(-1)])
    shard_len = mean_old.shape[0]
    size_x = lax.axis_size("gx")
    size_y = lax.axis_size("gy")
    size_z = lax.axis_size("gz")
    grad_grid = grad_flat.reshape(size_x, size_y, size_z, shard_len)
    curv_grid = curv_flat.reshape(size_x, size_y, size_z, shard_len)
    grad_grid, curv_grid = side_by_side((grad_grid, curv_grid), "gx", 0, 1)
    grad_grid, curv_grid = side_by_side_2((grad_grid, curv_grid), "gy", 1, 0)
    grad_grid, curv_grid = side_by_side_2((grad_grid, curv_grid), "gz", 2, 0)
    grad = grad_grid.reshape(shard_len)
    curv = curv_grid.reshape(shard_len)
    prec_new = 0.5 * prec_old + 0.5 * curv
    mom_new = 0.9 * mom_old + grad + 0.1 * mean_old
    divisor = prec_new + 0.1 + 0.05
    mean_new = mean_old - 0.3 * mom_new / divisor
    spread = jnp.sqrt(0.3 / divisor)
    posterior = jnp.stack([mean_new, spread])
    noise_row = noise[0]
    partial_z = gathered_copies(posterior, "gz", 1)
    partial_y = gathered_copies(partial_z, "gy", 1)
    piece = lax.all_gather(partial_y, "gx", axis=1, tiled=True)
    normal = noise_row.astype(jnp.float32)
    sample_row = (piece[0] + piece[1] * normal).astype(jnp.bfloat16)
    return (mean_new, prec_new, mom_new, sample_row.reshape(1, -1))


def solution(mesh):
    placed = (
        P(("gx", "gy", "gz"), None),
        P(("gx", "gy", "gz"), None),
        P(("gx", "gy", "gz"), None),
        P(("gx", "gy", "gz"), None),
        P(("gx", "gy", "gz")),
        P(("gx", "gy", "gz")),
        P(("gx", "gy", "gz")),
        P(("gx", "gy", "gz"), None),
    )
    return jax.shard_map(
        on_device,
        mesh=mesh,
        in_specs=placed,
        out_specs=(
            P(("gx", "gy", "gz")),
            P(("gx", "gy", "gz")),
            P(("gx", "gy", "gz")),
            P(("gx", "gy", "gz"), None),
        ),
        check_vma=False,
    )
```

profile of v0, /device:TPU:1, one launch (start us, length us, event | category | flops | bytes accessed | tf_op | source)
XLA Modules:
  0.0 272.1 jit_solution(154129348418022559)
XLA Ops:
  7.2 0.0 copy-start.3
  7.2 0.0 copy-start
  7.2 0.0 all-reduce.3.cloned.1.call-start
  7.2 1.8 fusion.5
  9.1 2.8 %fusion.2 = f32[1024,256]{1,0:T(8,128)} fusion(bf16[512,1024]{1,0:T(8,128)(2,1)} %param.8, bf16[512,256]{1,0:T(8,128)(2,1)} %param.9), kind=kOutput, calls=%fused_computation.6 | convolution fusion | flops 270401536 | bytes 2359296 | tf_op jit(solution)/shard_map/dot_general | solution.py:58
  11.8 0.0 copy-done.3
  11.8 0.0 copy-done
  11.8 0.5 fusion.6
  12.3 1.4 fusion.3
  13.7 0.0 copy-start.1
  13.7 1.3 concatenate.23
  15.0 1.5 concatenate.26
  16.6 0.0 copy-done.1
  16.6 1.7 maximum_maximum_fusion
  18.3 2.3 copy.24
  20.6 0.0 all-reduce.3.cloned.1.call-update
  20.6 0.0 all-gather.2.cloned.1.call-start
  20.6 1.3 dynamic-slice
  21.9 107.8 %all-reduce.3.cloned.1.call-done = f32[4,8,32,1024]{3,2,0,1:T(8,128)} async-done(((f32[4,8,32,1024]{3,2,0,1:T(8,128)}), f32[4,8,32,1024]{3,2,0,1:T(8,128)}) %all-reduce.3.cloned.1.call-update) | async-done | bytes 4194320
  129.7 0.0 copy-start.6
  129.7 0.0 copy-start.7
  129.7 0.0 copy-start.8
  129.7 2.0 constant_dynamic-slice_fusion
  131.7 0.1 maximum_bitcast_fusion
  131.8 16.8 %all_to_all.20 = f32[4,2,1,32,1024]{4,3,1,2,0:T(8,128)S(1)} all-to-all(f32[4,2,1,32,1024]{4,3,1,2,0:T(8,128)S(1)} %maximum_bitcast_fusion), channel_id=1, replica_groups=mesh['gx'=4,'gy'=4,'gz'=32] {'gy'}, dimensions={0} | all-to-all | bytes 2097152 | tf_op jit(solution)/shard_map/all_to_all | solution.py:24
  148.7 0.0 copy-start.2
  148.7 0.1 reduce_sum.18
  148.7 0.2 copy.21
  149.0 24.4 %all_to_all.21 = f32[32,2,1,1,1024]{4,1,3,2,0:T(2,128)S(1)} all-to-all(f32[32,2,1,1,1024]{4,1,3,2,0:T(2,128)S(1)} %copy.21), channel_id=1, replica_groups=mesh['gx'=4,'gy'=4,'gz'=32] {'gz'}, dimensions={0} | all-to-all | bytes 524288 | tf_op jit(solution)/shard_map/all_to_all | solution.py:24
  173.3 0.1 reduce_sum.19
  173.4 0.0 copy-done.6
  173.5 0.0 copy-start.4
  173.5 0.0 copy-done.7
  173.5 0.0 copy-done.8
  173.5 0.6 divide_subtract_fusion
  174.1 0.0 copy-start.5
  174.1 0.1 broadcast_in_dim.6
  174.2 17.3 %all_to_all.22 = f32[32,2,1024]{2,1,0:T(2,128)S(1)} all-to-all(f32[32,2,1024]{2,1,0:T(2,128)S(1)} %broadcast_in_dim.6), channel_id=1, replica_groups=mesh['gx'=4,'gy'=4,'gz'=32] {'gz'}, dimensions={0} | all-to-all | bytes 524288 | tf_op jit(solution)/shard_map/all_to_all | solution.py:45
  191.5 0.3 broadcast_in_dim.15
  191.7 20.3 %all_to_all.23 = f32[4,2,32768]{2,1,0:T(2,128)} all-to-all(f32[4,2,32768]{2,1,0:T(2,128)S(1)} %broadcast_in_dim.15), channel_id=1, replica_groups=mesh['gx'=4,'gy'=4,'gz'=32] {'gy'}, dimensions={0} | all-to-all | bytes 2097152 | tf_op jit(solution)/shard_map/all_to_all | solution.py:45
  212.0 0.0 all-gather.2.cloned.1.call-update
  212.0 45.2 %all-gather.2.cloned.1.call-done = f32[2,524288]{1,0:T(2,128)} async-done(((f32[2,131072]{1,0:T(2,128)}), f32[2,524288]{1,0:T(2,128)}) %all-gather.2.cloned.1.call-update) | async-done | bytes 4194320 | tf_op jit(solution)/shard_map/all_gather | solution.py:90
  257.2 0.0 copy-done.2
  257.2 8.1 %fusion.1 = bf16[1,524288]{1,0:T(2,128)(2,1)} fusion(bf16[1,524288]{1,0:T(2,128)(2,1)S(1)} %copy-done.2, f32[2,524288]{1,0:T(2,128)} %all-gather.2.cloned.1.call-done), kind=kLoop, calls=%fused_computation.5 | loop fusion | flops 2097152 | bytes 6291456 | tf_op jit(solution)/shard_map/convert_element_type | solution.py:92
  265.3 0.0 copy-done.4
  265.3 0.0 copy-done.5
  (3 shorter events, 0.0 us)
Async XLA Ops:
  7.2 4.7 %copy-start.3 = (bf16[512,256]{1,0:T(8,128)(2,1)S(1)}, bf16[512,256]{1,0:T(8,128)(2,1)}, u32[]{:S(2)}) copy-start(bf16[512,256]{1,0:T(8,128)(2,1)} %param.10) | copy-start | bytes 786436
  7.2 4.6 %copy-start = (bf16[512,1024]{1,0:T(8,128)(2,1)S(1)}, bf16[512,1024]{1,0:T(8,128)(2,1)}, u32[]{:S(2)}) copy-start(bf16[512,1024]{1,0:T(8,128)(2,1)} %param.11) | copy-start | bytes 3145732
  7.2 122.5 %all-reduce.3.cloned.1.call-start = ((), (), s32[]{:S(2)}) async-start(), calls=%async_computation.5 | async-start | bytes 8388608
  13.7 2.8 %copy-start.1 = (f32[256,1024]{1,0:T(8,128)S(1)}, f32[256,1024]{1,0:T(8,128)}, u32[]{:S(2)}) copy-start(f32[256,1024]{1,0:T(8,128)} %fusion.3) | copy-start | bytes 3145732
  20.6 236.6 %all-gather.2.cloned.1.call-start = ((), (), s32[]{:S(2)}) async-start(), calls=%async_computation.4 | async-start | bytes 5242880 | tf_op jit(solution)/shard_map/all_gather | solution.py:90
  129.7 43.7 %copy-start.6 = (f32[1024]{0:T(1024)S(1)}, f32[1024]{0:T(1024)}, u32[]{:S(2)}) copy-start(f32[1024]{0:T(1024)} %param.13) | copy-start | bytes 12292
  129.7 43.7 %copy-start.7 = (f32[1024]{0:T(1024)S(1)}, f32[1024]{0:T(1024)}, u32[]{:S(2)}) copy-start(f32[1024]{0:T(1024)} %param.12) | copy-start | bytes 12292
  129.7 43.8 %copy-start.8 = (f32[1024]{0:T(1024)S(1)}, f32[1024]{0:T(1024)}, u32[]{:S(2)}) copy-start(f32[1024]{0:T(1024)} %param.14) | copy-start | bytes 12292
  148.7 108.5 %copy-start.2 = (bf16[1,524288]{1,0:T(2,128)(2,1)S(1)}, bf16[1,524288]{1,0:T(2,128)(2,1)}, u32[]{:S(2)}) copy-start(bf16[1,524288]{1,0:T(2,128)(2,1)} %param.15) | copy-start | bytes 3145732
  173.5 91.8 %copy-start.4 = (f32[1024]{0:T(1024)}, f32[1024]{0:T(1024)S(1)}, u32[]{:S(2)}) copy-start(f32[1024]{0:T(1024)S(1)} %get-tuple-element.5) | copy-start | bytes 12292
  174.1 91.2 %copy-start.5 = (f32[1024]{0:T(1024)}, f32[1024]{0:T(1024)S(1)}, u32[]{:S(2)}) copy-start(f32[1024]{0:T(1024)S(1)} %get-tuple-element.6) | copy-start | bytes 12292
Sparse Core Ops, SparseCore 0:
  20.7 108.9 all-reduce.2
  212.1 45.0 all-gather.1
where the time goes:
time: 273 us; the launch traced here: 272 us
  waiting for transfers between devices  153 us (56%)
  blocking collectives  78.7 us (29%)
  between operations  14.2 us (5%)
  other arithmetic  10.7 us (4%)
  local copies, waits for them, and re-layouts  8.96 us (3%)
  matrix products  6.48 us (2%)
    unnamed x3, waiting for transfers between devices  108 us
    all_gather x1, waiting for transfers between devices, on_device(): piece = lax.all_gather(partial_y, 'gx', axis=1, tiled=True)  45.2 us
    all_to_all x2, blocking collectives, summed_on_arrival(): lax.all_to_all(pieces, axis, split_axis=0, concat_axis=0, tiled=True)  41.2 us
    all_to_all x2, blocking collectives, from_everyone(): lax.all_to_all(jnp.broadcast_to(x[None], (length, *x.shape)), axis, 0, 0,...  37.5 us
    convert_element_type x1, other arithmetic, on_device(): sample_row = (piece[0] + piece[1] * normal).astype(jnp.bfloat16)  8.07 us
    dot_general x4, matrix products, contract_rows(): lax.dot_general(left, right, (((0,), (0,)), ((), ())), preferred_element_...  6.48 us
  transfers between devices with their start and end apart: 2, of which 2 were waited for; matrix products, arithmetic and copies ran while one was open for 0% of the time, Pallas kernels for 0%

commit v1 on v0

v1 whole, which is shorter than its diff:
```python
import functools

import numpy as np
import jax
import jax.numpy as jnp
from jax import lax
from jax.experimental import pallas as pl
from jax.experimental.pallas import tpu as pltpu
from jax.sharding import PartitionSpec as P

AXES = ("gx", "gy", "gz")
DEVICES = 512
SHARD = 1024
HALF = DEVICES // 2


def place(i):
    gx, gy, gz = i // 128, (i // 32) % 4, i % 32
    x, y, z = gx, gz % 8, (gz // 8) * 2 + gy // 2
    y1, z1 = (y + 1) % 8, (z + 1) % 8
    return {
        "c": gy % 2,
        "a": ((x + 1) >> 1) & 1, "b": x >> 1,
        "yh": y >> 1, "yl": y & 1, "zh": z >> 1, "zl": z & 1,
        "Yh": y1 >> 1, "Yl": y1 & 1, "Zh": z1 >> 1, "Zl": z1 & 1,
    }


PLACES = [place(i) for i in range(DEVICES)]
STAGES = (
    (("a", "yl", "zl"), ("b", "yh"), ("zh",)),
    (("b", "Yl", "Zl"), ("a", "Zh"), ("Yh",)),
)


def stage_groups(stage):
    groups = {}
    for i, p in enumerate(PLACES):
        digits = STAGES[p["c"]]
        rest = [d for s, ds in enumerate(digits) if s != stage for d in ds]
        key = (p["c"],) + tuple(p[d] for d in rest)
        groups.setdefault(key, []).append((tuple(p[d] for d in digits[stage]), i))
    return [[i for _, i in sorted(members)] for members in groups.values()]


GROUPS = [stage_groups(s) for s in range(3)]
ORDER = [
    [
        i
        for _, i in sorted(
            (tuple(p[d] for ds in STAGES[c] for d in ds), i)
            for i, p in enumerate(PLACES)
            if p["c"] == c
        )
    ]
    for c in range(2)
]
PARTNER = [(i, (i // 64) * 64 + (i + 32) % 64) for i in range(DEVICES)]


def selectors():
    first = np.zeros((2, 4, 128, 1024), np.float32)
    third = np.zeros((2, 128, 256), np.float32)
    for c in range(2):
        rows = [n for n in ORDER[c] if n < HALF]
        for r, n in enumerate(rows):
            for q in range(4):
                first[c, q, r, 4 * n + q] = 1
        rows = [n - HALF for n in ORDER[c] if n >= HALF]
        for r, n in enumerate(rows):
            third[c, r, n] = 1
    return first.reshape(2, 512, 1024), third


def mm(a, b, dims=((1,), (0,))):
    return lax.dot_general(a, b, (dims, ((), ())), preferred_element_type=jnp.float32)


def half_kernel(half_ref, in_first, cot_first, in_third, cot_third, pick_first, pick_third, out):
    half = half_ref[0]

    def base(b, g):
        return pl.multiple_of(jnp.where(half == 0, g * 32 + b * 16, b * 128 + g * 16), 16)

    def squares(v):
        return (v * v).astype(jnp.bfloat16)

    wide = cot_third[...].astype(jnp.float32)
    rows = mm(pick_third[0], in_third[...], ((1,), (1,)))
    grad = mm(rows.astype(jnp.bfloat16), cot_third[...])
    curv = mm(squares(rows), squares(wide))
    for g in range(8):
        out[pl.ds(base(1, g), 16), 0:1024] = grad[16 * g : 16 * g + 16]
        out[pl.ds(base(1, g), 16), 1024:2048] = curv[16 * g : 16 * g + 16]
    wide = cot_first[...].astype(jnp.float32)
    cot_sq = squares(wide)
    for q in range(4):
        rows = mm(pick_first[0, 128 * q : 128 * q + 128], in_first[...], ((1,), (1,)))
        grad = mm(rows.astype(jnp.bfloat16), cot_first[...])
        curv = mm(squares(rows), cot_sq)
        for g in range(8):
            out[pl.ds(base(0, g), 16), 256 * q : 256 * q + 256] = grad[16 * g : 16 * g + 16]
            out[pl.ds(base(0, g), 16), 1024 + 256 * q : 1280 + 256 * q] = curv[16 * g : 16 * g + 16]


def half_sums(half, in_first, cot_first, in_third, cot_third, pick_first, pick_third):
    def whole(*shape):
        return pl.BlockSpec(shape, lambda i, s: (0,) * len(shape))

    return pl.pallas_call(
        half_kernel,
        grid_spec=pltpu.PrefetchScalarGridSpec(
            num_scalar_prefetch=1,
            grid=(1,),
            in_specs=[
                whole(512, 1024), whole(512, 256), whole(512, 256), whole(512, 1024),
                pl.BlockSpec((1, 512, 1024), lambda i, s: (s[0], 0, 0)),
                pl.BlockSpec((1, 128, 256), lambda i, s: (s[0], 0, 0)),
            ],
            out_specs=whole(256, 2048),
        ),
        out_shape=jax.ShapeDtypeStruct((256, 2048), jnp.float32),
        compiler_params=pltpu.CompilerParams(vmem_limit_bytes=32 * 1024 * 1024),
        cost_estimate=pl.CostEstimate(flops=1_100_000_000, bytes_accessed=5_600_000, transcendentals=0),
        name="half_sums",
    )(half, in_first, cot_first, in_third, cot_third, pick_first, pick_third)


def order_kernel(core_ref, table, own, other, mean, spread):
    core = core_ref[0]

    def step(p, carry):
        mine, theirs = table[core, p], table[1 - core, p]
        mean[mine] = own[p, 0]
        spread[mine] = own[p, 1]
        mean[theirs] = other[p, 0]
        spread[theirs] = other[p, 1]
        return carry

    lax.fori_loop(0, HALF, step, 0, unroll=8)


def in_flat_order(core, own, other):
    table = jnp.asarray(np.array(ORDER, np.int32))
    shape = jax.ShapeDtypeStruct((DEVICES, 8, 128), jnp.float32)
    smem = pl.BlockSpec(memory_space=pltpu.SMEM)
    return pl.pallas_call(
        order_kernel,
        in_specs=[smem, smem, pl.BlockSpec(memory_space=pltpu.VMEM), pl.BlockSpec(memory_space=pltpu.VMEM)],
        out_specs=[pl.BlockSpec(memory_space=pltpu.VMEM)] * 2,
        out_shape=[shape, shape],
        compiler_params=pltpu.CompilerParams(vmem_limit_bytes=32 * 1024 * 1024),
        name="flat_order",
    )(core, table, own, other)


def exchanged(x, groups):
    return lax.all_to_all(x, AXES, 0, 0, axis_index_groups=groups, tiled=True)


def summed(x, groups):
    return exchanged(x, groups).sum(axis=0)


def from_all(x, groups):
    return exchanged(jnp.broadcast_to(x[None], (len(groups[0]), *x.shape)), groups)


def on_device(in_first, cot_first, in_third, cot_third, mean_old, prec_old, mom_old, noise):
    core = lax.axis_index("gy") % 2
    gz = lax.axis_index("gz")
    slot = jnp.where(core == 0, gz // 8, ((gz % 8 + 1) % 8) // 2)
    first, third = selectors()
    first, third = jnp.asarray(first, jnp.bfloat16), jnp.asarray(third, jnp.bfloat16)
    core_1 = core.astype(jnp.int32).reshape(1)
    send = half_sums(1 - core_1, in_first, cot_first, in_third, cot_third, first, third)
    arrived = lax.ppermute(send, AXES, PARTNER)
    keep = half_sums(core_1, in_first, cot_first, in_third, cot_third, first, third)
    sums = (keep + arrived).reshape(8, 32, 2048)
    sums = summed(sums, GROUPS[0]).reshape(8, 4, 2048)
    sums = summed(sums, GROUPS[1])
    state = jnp.concatenate([mean_old, prec_old, mom_old, mom_old]).reshape(2, 2048)
    parts = from_all(jnp.concatenate([sums, state, state], axis=0), GROUPS[2])
    total = parts[:, :4].sum(axis=0)
    grad, curv = total[:, :1024], total[:, 1024:]
    mean_4, prec_4, mom_4 = parts[:, 4, :1024], parts[:, 4, 1024:], parts[:, 5, :1024]
    prec_new = 0.5 * prec_4 + 0.5 * curv
    mom_new = 0.9 * mom_4 + grad + 0.1 * mean_4
    divisor = prec_new + 0.1 + 0.05
    mean_new = mean_4 - 0.3 * mom_new / divisor
    spread = jnp.sqrt(0.3 / divisor)
    posterior = jnp.stack([mean_new.reshape(4, 8, 128), spread.reshape(4, 8, 128)], axis=1)
    mine = [lax.dynamic_index_in_dim(v, slot, 0, keepdims=False) for v in (mean_new, prec_new, mom_new)]
    block = from_all(posterior, GROUPS[1]).reshape(32, 2, 8, 128)
    own = from_all(block, GROUPS[0]).reshape(256, 2, 8, 128)
    other = lax.ppermute(own, AXES, PARTNER)
    mean, spread = in_flat_order(core_1, own, other)
    sample_row = (mean.reshape(1, -1) + spread.reshape(1, -1) * noise.astype(jnp.float32)).astype(jnp.bfloat16)
    return (*mine, sample_row)


def solution(mesh):
    rows, flat = P(AXES, None), P(AXES)
    return jax.shard_map(
        on_device,
        mesh=mesh,
        in_specs=(rows, rows, rows, rows, flat, flat, flat, rows),
        out_specs=(flat, flat, flat, rows),
        check_vma=False,
    )
```

time: 273 us -> 127 us (0.47)
  waiting for transfers between devices: 153 us -> 12 us
  starting transfers between devices: 0.08 us -> 17.2 us
  between operations: 14.2 us -> 0.93 us
  Pallas kernels: 0 us -> 8.68 us
  matrix products: 6.48 us -> 0 us
  other arithmetic: 10.7 us -> 5.06 us
  blocking collectives: 78.7 us -> 73.4 us
    unnamed x3 -> x0, waiting for transfers between devices: 108 us -> none
    all_gather x1 -> x0, waiting for transfers between devices: 45.2 us -> none  [on_device(): piece = lax.all_gather(partial_y, 'gx', axis=1, tiled=True)]
    ppermute x0 -> x2, starting transfers between devices: none -> 13.6 us  [the longest x1 8.79 us: on_device(): arrived = lax.ppermute(send, AXES, PARTNER)]
    pallas_call x0 -> x3, Pallas kernels: none -> 8.68 us  [the longest x2 5.38 us: half_sums(): pl.pallas_call(half_kernel, grid_spec=pltpu.PrefetchScalarGridSpec(num_sc...]
    all_to_all x0 -> x1, waiting for transfers between devices: none -> 8.38 us  [exchanged(): return lax.all_to_all(x, AXES, 0, 0, axis_index_groups=groups, tiled=True)]
    dot_general x4 -> x0, matrix products: 6.48 us -> none  [contract_rows(): lax.dot_general(left, right, (((0,), (0,)), ((), ())), preferred_element_...]
    unnamed x19 -> x28, local copies, waits for them, and re-layouts: 1.31 us -> 6.87 us
    all_to_all x4, blocking collectives: 78.7 us -> 73.4 us  [exchanged(): return lax.all_to_all(x, AXES, 0, 0, axis_index_groups=groups, tiled=True)]
  transfers between devices with their start and end apart: 2 -> 3, of which waited for: 2 -> 3; matrix products, arithmetic and copies ran while one was open for 0% -> 1% of each run, Pallas kernels for 0% -> 2%
where the time goes in v1:
time: 127 us; the launch traced here: 126 us
  blocking collectives  73.4 us (58%)
  starting transfers between devices  17.2 us (14%)
  waiting for transfers between devices  12 us (9%)
  local copies, waits for them, and re-layouts  9.13 us (7%)
  Pallas kernels  8.68 us (7%)
  other arithmetic  5.06 us (4%)
    all_to_all x4, blocking collectives, exchanged(): return lax.all_to_all(x, AXES, 0, 0, axis_index_groups=groups, tiled=True)  73.4 us
    ppermute x1, starting transfers between devices, on_device(): arrived = lax.ppermute(send, AXES, PARTNER)  8.79 us
    all_to_all x1, waiting for transfers between devices, exchanged(): return lax.all_to_all(x, AXES, 0, 0, axis_index_groups=groups, tiled=True)  8.38 us
    unnamed x28, local copies, waits for them, and re-layouts  6.87 us
    pallas_call x2, Pallas kernels, half_sums(): pl.pallas_call(half_kernel, grid_spec=pltpu.PrefetchScalarGridSpec(num_sc...  5.38 us
    ppermute x1, starting transfers between devices, on_device(): other = lax.ppermute(own, AXES, PARTNER)  4.78 us
    convert_element_type x1, other arithmetic, on_device(): (mean.reshape(1, -1) + spread.reshape(1, -1) * noise.astype(jnp.float32))...  4.46 us
    all_to_all x1, starting transfers between devices, exchanged(): return lax.all_to_all(x, AXES, 0, 0, axis_index_groups=groups, tiled=True)  3.64 us
  transfers between devices with their start and end apart: 3, of which 3 were waited for; matrix products, arithmetic and copies ran while one was open for 1% of the time, Pallas kernels for 2%

profile of v1, /device:TPU:1, one launch (start us, length us, event | category | flops | bytes accessed | tf_op | source)
XLA Modules:
  0.0 126.4 jit_solution(11605886479416611212)
XLA Ops:
  0.6 0.0 copy-start
  0.7 1.6 %copy-done = bf16[2,512,1024]{2,1,0:T(8,128)(2,1)S(1)} copy-done((bf16[2,512,1024]{2,1,0:T(8,128)(2,1)S(1)}, bf16[2,512,1024]{2,1,0:T(8,128)(2,1)}, u32[]{:S(2)}) %copy-start) | copy-done | bytes 2097176
  2.2 0.0 copy-start.2
  2.2 1.2 copy-done.2
  3.5 0.0 copy-start.4
  3.5 1.2 copy-done.4
  4.7 0.0 copy-start.6
  4.7 0.9 copy-done.6
  5.6 0.0 copy-start.7
  5.6 0.9 copy-done.7
  6.6 0.0 copy-start.8
  6.6 0.9 copy-done.8
  7.5 0.0 copy-start.1
  7.5 0.0 copy-start.3
  7.5 0.0 copy-start.5
  7.5 2.7 %half_sums.3 = f32[256,2048]{1,0:T(8,128)S(1)} custom-call(s32[1]{0:T(128)S(6)} %sub.13.half_ref, bf16[512,1024]{1,0:T(8,128)(2,1)S(1)} %copy-done.2, bf16[512,256]{1,0:T(8,128)(2,1)S(1)} %copy-done.6, bf16[512,256]{1,0:T(8,128)(2,1)S(1)} %copy-done.7, bf16[512,1024]{1,0:T(8,128)(2,1)S(1)} %copy-done.4, bf16[2,512,1024]{2,1,0:T(8,128)(2,1)S(1)} %copy-done, ...), custom_call_target="tpu_custom_call" | custom-call | flops 1100000000 | bytes 5600000 | tf_op jit(solution)/shard_map/half_sums/pallas_call | solution.py:110
  10.2 8.8 %collective-permute-start = (f32[256,2048]{1,0:T(8,128)S(1)}, f32[256,2048]{1,0:T(8,128)S(1)}, u32[]{:S(2)}, u32[]{:S(2)}) collective-permute-start(f32[256,2048]{1,0:T(8,128)S(1)} %half_sums.3), channel_id=1, source_target_pairs={{0,32},{1,33},{2,34},{3,35},{4,36},{5,37},{6,38},{7,39},{8,40},{9,... | collective-permute-start | bytes 6291464 | tf_op jit(solution)/shard_map/ppermute | solution.py:177
  19.0 0.0 copy-done.1
  19.0 0.0 copy-done.3
  19.0 0.0 copy-done.5
  19.0 2.7 %half_sums.2 = f32[256,2048]{1,0:T(8,128)S(1)} custom-call(s32[1]{0:T(128)} %bitcast.half_ref.core_ref, bf16[512,1024]{1,0:T(8,128)(2,1)S(1)} %copy-done.3, bf16[512,256]{1,0:T(8,128)(2,1)S(1)} %copy-done.6, bf16[512,256]{1,0:T(8,128)(2,1)S(1)} %copy-done.7, bf16[512,1024]{1,0:T(8,128)(2,1)S(1)} %copy-done.5, bf16[2,512,1024]{2,1,0:T(8,128)(2,1)S(1)} %copy-done.1, ...), custom_call_target="tpu_custom_call" | custom-call | flops 1100000000 | bytes 5600000 | tf_op jit(solution)/shard_map/half_sums/pallas_call | solution.py:110
  21.7 1.0 collective-permute-done
  22.8 0.3 add.47
  23.1 24.6 %all_to_all.25 = f32[8,32,2048]{2,1,0:T(8,128)S(1)} all-to-all(f32[8,32,2048]{2,1,0:T(8,128)S(1)} %bitcast.39), channel_id=1, replica_groups={{0,64,1,65,128,192,129,193},{2,66,3,67,130,194,131,195},{4,68,5,69,132,..., dimensions={0} | all-to-all | bytes 4194304 | tf_op jit(solution)/shard_map/all_to_all | solution.py:158
  47.7 0.0 copy-start.11
  47.7 0.0 copy-start.12
  47.7 0.0 copy-start.13
  47.7 0.1 reduce_sum.27
  47.8 0.8 reshape.36
  48.6 3.6 %all-to-all-start.1 = ((f32[8,4,2048]{2,1,0:T(4,128)}), f32[8,4,2048]{2,1,0:T(4,128)S(1)}, u32[]{:S(2)}, u32[]{:S(2)}) async-start(f32[8,4,2048]{2,1,0:T(4,128)} %reshape.36), calls=%async_computation.1 | async-start | bytes 524288 | tf_op jit(solution)/shard_map/all_to_all | solution.py:158
  52.2 0.0 copy-done.11
  52.2 0.0 copy-done.12
  52.3 0.0 copy-done.13
  52.3 8.4 %all-to-all-done.1 = f32[8,4,2048]{2,1,0:T(4,128)S(1)} async-done(((f32[8,4,2048]{2,1,0:T(4,128)}), f32[8,4,2048]{2,1,0:T(4,128)S(1)}, u32[]{:S(2)}, u32[]{:S(2)}) %all-to-all-start.1) | async-done | bytes 262176 | tf_op jit(solution)/shard_map/all_to_all | solution.py:158
  60.8 14.1 %all_to_all.26 = f32[4,8,2048]{2,1,0:T(8,128)S(1)} all-to-all(f32[4,8,2048]{2,1,0:T(8,128)S(1)} %broadcast_in_dim.8), channel_id=1, replica_groups={{0,8,16,24},{1,9,17,25},{2,10,18,26},{3,11,19,27},{4,12,20,28},{5,13,21..., dimensions={0} | all-to-all | bytes 524288 | tf_op jit(solution)/shard_map/all_to_all | solution.py:158
  75.1 12.3 %all_to_all.27 = f32[8,4,2,8,128]{4,3,2,1,0:T(8,128)S(1)} all-to-all(f32[8,4,2,8,128]{4,3,2,1,0:T(8,128)S(1)} %broadcast_in_dim.9), channel_id=1, replica_groups={{0,2,4,6,384,386,388,390},{1,3,5,7,385,387,389,391},{8,10,12,14,392,394..., dimensions={0} | all-to-all | bytes 524288 | tf_op jit(solution)/shard_map/all_to_all | solution.py:158
  87.4 0.2 broadcast_in_dim.22
  87.6 0.0 copy-start.9
  87.6 22.3 %all_to_all.28 = f32[8,32,2,8,128]{4,3,2,1,0:T(8,128)S(1)} all-to-all(f32[8,32,2,8,128]{4,3,2,1,0:T(8,128)S(1)} %broadcast_in_dim.22), channel_id=1, replica_groups={{0,64,1,65,128,192,129,193},{2,66,3,67,130,194,131,195},{4,68,5,69,132,..., dimensions={0} | all-to-all | bytes 4194304 | tf_op jit(solution)/shard_map/all_to_all | solution.py:158
  109.9 4.8 %collective-permute-start.1 = (f32[256,2,8,128]{3,2,1,0:T(8,128)S(1)}, f32[256,2,8,128]{3,2,1,0:T(8,128)}, u32[]{:S(2)}, u32[]{:S(2)}) collective-permute-start(f32[256,2,8,128]{3,2,1,0:T(8,128)S(1)} %bitcast.35), channel_id=1, source_target_pairs={{0,32},{1,33},{2,34},{3,35},{4,36},{5,37},{6,38},{7,39},{8,40},{9,... | collective-permute-start | bytes 6291464 | tf_op jit(solution)/shard_map/ppermute | solution.py:196
  114.8 0.6 constant_dynamic-slice_fusion.1
  115.4 0.6 constant_dynamic-slice_fusion
  116.0 0.0 copy-start.10
  116.0 2.6 %collective-permute-done.1.other = f32[256,2,8,128]{3,2,1,0:T(8,128)} collective-permute-done((f32[256,2,8,128]{3,2,1,0:T(8,128)S(1)}, f32[256,2,8,128]{3,2,1,0:T(8,128)}, u32[]{:S(2)}, u32[]{:S(2)}) %collective-permute-start.1) | collective-permute-done | bytes 2097184 | tf_op jit(solution)/shard_map/ppermute | solution.py:196
  118.6 0.0 copy-done.9
  118.6 3.3 %flat_order.1 = (f32[512,8,128]{2,1,0:T(8,128)S(1)}, f32[512,8,128]{2,1,0:T(8,128)S(1)}) custom-call(s32[1]{0:T(128)} %bitcast.half_ref.core_ref, s32[2,256]{1,0:T(2,128)S(1)} %copy-done.9, f32[256,2,8,128]{3,2,1,0:T(8,128)S(1)} %bitcast.36, f32[256,2,8,128]{3,2,1,0:T(8,128)} %collective-permute-done.1.other), custom_call_target="tpu_custom_call" | custom-call | tf_op jit(solution)/shard_map/flat_order/pallas_call | solution.py:147
  121.9 0.0 copy-done.10
  121.9 4.5 %add_convert_fusion = bf16[1,524288]{1,0:T(2,128)(2,1)} fusion(f32[1,524288]{1,0:T(1,128)S(1)} %bitcast.37, f32[1,524288]{1,0:T(1,128)S(1)} %bitcast.38, bf16[1,524288]{1,0:T(2,128)(2,1)S(1)} %copy-done.10), kind=kLoop, calls=%fused_computation | loop fusion | flops 2097152 | bytes 6291456 | tf_op jit(solution)/shard_map/convert_element_type | solution.py:198
  (13 shorter events, 0.3 us)
Async XLA Ops:
  0.6 1.6 %copy-start = (bf16[2,512,1024]{2,1,0:T(8,128)(2,1)S(1)}, bf16[2,512,1024]{2,1,0:T(8,128)(2,1)}, u32[]{:S(2)}) copy-start(bf16[2,512,1024]{2,1,0:T(8,128)(2,1)} %constant.88.clone.pick_first) | copy-start | bytes 6291460
  2.2 1.2 copy-start.2
  3.5 1.2 copy-start.4
  4.7 0.9 copy-start.6
  5.6 0.9 copy-start.7
  6.6 0.9 copy-start.8
  7.5 11.5 %copy-start.1 = (bf16[2,512,1024]{2,1,0:T(8,128)(2,1)S(1)}, bf16[2,512,1024]{2,1,0:T(8,128)(2,1)}, u32[]{:S(2)}) copy-start(bf16[2,512,1024]{2,1,0:T(8,128)(2,1)} %constant.88.clone.pick_first) | copy-start | bytes 6291460
  7.5 11.5 %copy-start.3 = (bf16[512,1024]{1,0:T(8,128)(2,1)S(1)}, bf16[512,1024]{1,0:T(8,128)(2,1)}, u32[]{:S(2)}) copy-start(bf16[512,1024]{1,0:T(8,128)(2,1)} %in_first.3) | copy-start | bytes 3145732
  7.5 11.5 %copy-start.5 = (bf16[512,1024]{1,0:T(8,128)(2,1)S(1)}, bf16[512,1024]{1,0:T(8,128)(2,1)}, u32[]{:S(2)}) copy-start(bf16[512,1024]{1,0:T(8,128)(2,1)} %cot_third.3) | copy-start | bytes 3145732
  10.2 12.6 %collective-permute-start = (f32[256,2048]{1,0:T(8,128)S(1)}, f32[256,2048]{1,0:T(8,128)S(1)}, u32[]{:S(2)}, u32[]{:S(2)}) collective-permute-start(f32[256,2048]{1,0:T(8,128)S(1)} %half_sums.3), channel_id=1, source_target_pairs={{0,32},{1,33},{2,34},{3,35},{4,36},{5,37},{6,38},{7,39},{8,40},{9,... | collective-permute-start | bytes 6291464 | tf_op jit(solution)/shard_map/ppermute | solution.py:177
  47.7 4.5 %copy-start.11 = (f32[1024]{0:T(1024)S(1)}, f32[1024]{0:T(1024)}, u32[]{:S(2)}) copy-start(f32[1024]{0:T(1024)} %param.17) | copy-start | bytes 12292
  47.7 4.5 %copy-start.12 = (f32[1024]{0:T(1024)S(1)}, f32[1024]{0:T(1024)}, u32[]{:S(2)}) copy-start(f32[1024]{0:T(1024)} %param.16) | copy-start | bytes 12292
  47.7 4.6 %copy-start.13 = (f32[1024]{0:T(1024)S(1)}, f32[1024]{0:T(1024)}, u32[]{:S(2)}) copy-start(f32[1024]{0:T(1024)} %param.15) | copy-start | bytes 12292
  48.6 12.1 %all-to-all-start.1 = ((f32[8,4,2048]{2,1,0:T(4,128)}), f32[8,4,2048]{2,1,0:T(4,128)S(1)}, u32[]{:S(2)}, u32[]{:S(2)}) async-start(f32[8,4,2048]{2,1,0:T(4,128)} %reshape.36), calls=%async_computation.1 | async-start | bytes 524288 | tf_op jit(solution)/shard_map/all_to_all | solution.py:158
  87.6 31.0 %copy-start.9 = (s32[2,256]{1,0:T(2,128)S(1)}, s32[2,256]{1,0:T(2,128)}, u32[]{:S(2)}) copy-start(s32[2,256]{1,0:T(2,128)} %constant.90.clone.table) | copy-start | bytes 6148
  109.9 8.7 %collective-permute-start.1 = (f32[256,2,8,128]{3,2,1,0:T(8,128)S(1)}, f32[256,2,8,128]{3,2,1,0:T(8,128)}, u32[]{:S(2)}, u32[]{:S(2)}) collective-permute-start(f32[256,2,8,128]{3,2,1,0:T(8,128)S(1)} %bitcast.35), channel_id=1, source_target_pairs={{0,32},{1,33},{2,34},{3,35},{4,36},{5,37},{6,38},{7,39},{8,40},{9,... | collective-permute-start | bytes 6291464 | tf_op jit(solution)/shard_map/ppermute | solution.py:196
  116.0 5.9 %copy-start.10 = (bf16[1,524288]{1,0:T(2,128)(2,1)S(1)}, bf16[1,524288]{1,0:T(2,128)(2,1)}, u32[]{:S(2)}) copy-start(bf16[1,524288]{1,0:T(2,128)(2,1)} %param.18) | copy-start | bytes 3145732

commit v2 on v1

v2 whole, which is shorter than its diff:
```python
import functools

import numpy as np
import jax
import jax.numpy as jnp
from jax import lax
from jax.experimental import pallas as pl
from jax.experimental.pallas import tpu as pltpu
from jax.sharding import PartitionSpec as P

AXES = ("gx", "gy", "gz")
DEVICES = 512
SHARD = 1024
HALF = DEVICES // 2


def place(i):
    gx, gy, gz = i // 128, (i // 32) % 4, i % 32
    x, y, z = gx, gz % 8, (gz // 8) * 2 + gy // 2
    y1, z1 = (y + 1) % 8, (z + 1) % 8
    return {
        "c": gy % 2,
        "a": ((x + 1) >> 1) & 1, "b": x >> 1,
        "yh": y >> 1, "yl": y & 1, "zh": z >> 1, "zl": z & 1,
        "Yh": y1 >> 1, "Yl": y1 & 1, "Zh": z1 >> 1, "Zl": z1 & 1,
    }


PLACES = [place(i) for i in range(DEVICES)]
STAGES = (
    (("a", "yl", "zl"), ("b", "yh"), ("zh",)),
    (("b", "Yl", "Zl"), ("a", "Zh"), ("Yh",)),
)


def stage_groups(stage):
    groups = {}
    for i, p in enumerate(PLACES):
        digits = STAGES[p["c"]]
        rest = [d for s, ds in enumerate(digits) if s != stage for d in ds]
        key = (p["c"],) + tuple(p[d] for d in rest)
        groups.setdefault(key, []).append((tuple(p[d] for d in digits[stage]), i))
    return [[i for _, i in sorted(members)] for members in groups.values()]


GROUPS = [stage_groups(s) for s in range(3)]
ORDER = [
    [
        i
        for _, i in sorted(
            (tuple(p[d] for ds in STAGES[c] for d in ds), i)
            for i, p in enumerate(PLACES)
            if p["c"] == c
        )
    ]
    for c in range(2)
]
PARTNER = [(i, (i // 64) * 64 + (i + 32) % 64) for i in range(DEVICES)]


def selectors():
    first = np.zeros((2, 4, 128, 1024), np.float32)
    third = np.zeros((2, 128, 256), np.float32)
    for c in range(2):
        rows = [n for n in ORDER[c] if n < HALF]
        for r, n in enumerate(rows):
            for q in range(4):
                first[c, q, r, 4 * n + q] = 1
        rows = [n - HALF for n in ORDER[c] if n >= HALF]
        for r, n in enumerate(rows):
            third[c, r, n] = 1
    return first.reshape(2, 512, 1024), third


def mm(a, b, dims=((1,), (0,))):
    return lax.dot_general(a, b, (dims, ((), ())), preferred_element_type=jnp.float32)


def half_body(half, in_first, cot_first, in_third, cot_third, pick_first, pick_third, out, ready):
    def base(b, g):
        return pl.multiple_of(jnp.where(half == 0, g * 32 + b * 16, b * 128 + g * 16), 16)

    def squares(v):
        return (v * v).astype(jnp.bfloat16)

    def spread_out(b, lane, width, grad, curv):
        for g in range(8):
            out[pl.ds(base(b, g), 16), lane : lane + width] = grad[16 * g : 16 * g + 16]
            out[pl.ds(base(b, g), 16), 1024 + lane : 1024 + lane + width] = curv[16 * g : 16 * g + 16]

    ready(0)
    rows = mm(pick_third[...], in_third[...], ((1,), (1,)))
    ready(1)
    wide = cot_third[...].astype(jnp.float32)
    grad = mm(rows.astype(jnp.bfloat16), cot_third[...])
    curv = mm(squares(rows), squares(wide))
    spread_out(1, 0, 1024, grad, curv)
    ready(2)
    wide = cot_first[...].astype(jnp.float32)
    cot_sq = squares(wide)
    for q in range(4):
        rows = mm(pick_first[128 * q : 128 * q + 128], in_first[...], ((1,), (1,)))
        grad = mm(rows.astype(jnp.bfloat16), cot_first[...])
        curv = mm(squares(rows), cot_sq)
        spread_out(0, 256 * q, 256, grad, curv)


def fetching_kernel(half_ref, in_first, cot_first, in_third, cot_third, pick_first, pick_third,
                    out, a, b, c, d, e, f, sems):
    half = half_ref[0]
    moves = [
        ((in_third, c), (pick_third.at[half], f)),
        ((cot_third, d),),
        ((cot_first, b), (in_first, a), (pick_first.at[half], e)),
    ]
    copies, at = [], 0
    for group in moves:
        copies.append([])
        for src, dst in group:
            copies[-1].append(pltpu.make_async_copy(src, dst, sems.at[at]))
            at += 1
    for group in copies:
        for copy in group:
            copy.start()

    def ready(stage):
        for copy in copies[stage]:
            copy.wait()

    half_body(half, a, b, c, d, e, f, out, ready)


def held_kernel(half_ref, in_first, cot_first, in_third, cot_third, pick_first, pick_third, out):
    half_body(half_ref[0], in_first, cot_first, in_third, cot_third, pick_first.at[0], pick_third.at[0],
              out, lambda stage: None)


SUMS = jax.ShapeDtypeStruct((256, 2048), jnp.float32)
COST = pl.CostEstimate(flops=1_100_000_000, bytes_accessed=5_600_000, transcendentals=0)
PARAMS = pltpu.CompilerParams(vmem_limit_bytes=32 * 1024 * 1024)
SMEM = pl.BlockSpec(memory_space=pltpu.SMEM)
VMEM = pl.BlockSpec(memory_space=pltpu.VMEM)
HBM = pl.BlockSpec(memory_space=pltpu.HBM)


def sums_to_send(half, *arrays):
    def buffer(*shape):
        return pltpu.VMEM(shape, jnp.bfloat16)

    return pl.pallas_call(
        fetching_kernel,
        in_specs=[SMEM] + [HBM] * 6,
        out_specs=VMEM,
        out_shape=SUMS,
        scratch_shapes=[
            buffer(512, 1024), buffer(512, 256), buffer(512, 256), buffer(512, 1024),
            buffer(512, 1024), buffer(128, 256), pltpu.SemaphoreType.DMA((6,)),
        ],
        compiler_params=pltpu.CompilerParams(vmem_limit_bytes=56 * 1024 * 1024),
        cost_estimate=COST,
        name="sums_to_send",
    )(half, *arrays)


def sums_to_keep(half, *arrays):
    def whole(*shape):
        return pl.BlockSpec(shape, lambda i, s: (0,) * len(shape))

    return pl.pallas_call(
        held_kernel,
        grid_spec=pltpu.PrefetchScalarGridSpec(
            num_scalar_prefetch=1,
            grid=(1,),
            in_specs=[
                whole(512, 1024), whole(512, 256), whole(512, 256), whole(512, 1024),
                pl.BlockSpec((1, 512, 1024), lambda i, s: (s[0], 0, 0)),
                pl.BlockSpec((1, 128, 256), lambda i, s: (s[0], 0, 0)),
            ],
            out_specs=whole(256, 2048),
        ),
        out_shape=SUMS,
        compiler_params=PARAMS,
        cost_estimate=COST,
        name="sums_to_keep",
    )(half, *arrays)


def sample_kernel(half_ref, table, noise, posterior, *refs):
    out, rows, sems = refs[-3:]
    half = half_ref[0]
    copies = []
    for run in range(8):
        first = (run >> 1) * 128 + (run & 1) * 64 + half * 32

        def step(j, carry, run=run, first=first):
            at = pl.ds(pl.multiple_of((first + j) * SHARD, SHARD), SHARD)
            p = table[half, run * 32 + j]
            normal = noise[0:1, at].astype(jnp.float32).reshape(8, 128)
            row = posterior[p, 0] + posterior[p, 1] * normal
            rows[0:1, at] = row.reshape(1, SHARD).astype(jnp.bfloat16)
            return carry

        lax.fori_loop(0, 32, step, 0, unroll=8)
        part = pl.ds(pl.multiple_of(first * SHARD, 32 * SHARD), 32 * SHARD)
        copies.append(pltpu.make_async_copy(rows.at[:, part], out.at[:, part], sems.at[run]))
        copies[-1].start()
    for copy in copies:
        copy.wait()


def sampled(half, noise, posterior, *begun):
    table = np.array([np.argsort(order) for order in ORDER], np.int32)
    return pl.pallas_call(
        sample_kernel,
        in_specs=[SMEM, SMEM, VMEM, VMEM] + [HBM] * len(begun),
        out_specs=HBM,
        out_shape=jax.ShapeDtypeStruct(noise.shape, jnp.bfloat16),
        scratch_shapes=[pltpu.VMEM(noise.shape, jnp.bfloat16), pltpu.SemaphoreType.DMA((8,))],
        input_output_aliases={4: 0} if begun else {},
        compiler_params=PARAMS,
        cost_estimate=pl.CostEstimate(flops=524288, bytes_accessed=4_200_000, transcendentals=0),
        name="sampled",
    )(half, jnp.asarray(table), noise, posterior, *begun)


def exchanged(x, groups):
    return lax.all_to_all(x, AXES, 0, 0, axis_index_groups=groups, tiled=True)


def summed(x, groups):
    return exchanged(x, groups).sum(axis=0)


def from_all(x, groups):
    return exchanged(jnp.broadcast_to(x[None], (len(groups[0]), *x.shape)), groups)


def on_device(in_first, cot_first, in_third, cot_third, mean_old, prec_old, mom_old, noise):
    core = lax.axis_index("gy") & 1
    gz = lax.axis_index("gz")
    slot = jnp.where(core == 0, gz >> 3, (((gz & 7) + 1) & 7) >> 1)
    first, third = selectors()
    arrays = (in_first, cot_first, in_third, cot_third, jnp.asarray(first, jnp.bfloat16), jnp.asarray(third, jnp.bfloat16))
    here = core.astype(jnp.int32).reshape(1)
    there = 1 - here
    send = sums_to_send(there, *arrays)
    arrived = lax.ppermute(send, AXES, PARTNER)
    keep = sums_to_keep(here, *arrays)
    state = jnp.concatenate([mean_old, prec_old, mom_old])
    state = jnp.where(jnp.arange(4)[:, None] == slot, state[None], 0.0)
    sums, state = lax.optimization_barrier((keep + arrived, state))
    sums = summed(sums.reshape(8, 32, 2048), GROUPS[0]).reshape(8, 4, 2048)
    sums = summed(sums, GROUPS[1])
    total = from_all(jnp.concatenate([sums, state], axis=1), GROUPS[2]).sum(axis=0)
    grad, curv, mean_4, prec_4, mom_4 = (total[:, 1024 * i : 1024 * (i + 1)] for i in range(5))
    prec_new = 0.5 * prec_4 + 0.5 * curv
    mom_new = 0.9 * mom_4 + grad + 0.1 * mean_4
    divisor = prec_new + 0.1 + 0.05
    mean_new = mean_4 - 0.3 * mom_new / divisor
    spread = jnp.sqrt(0.3 / divisor)
    posterior = jnp.stack([mean_new.reshape(4, 8, 128), spread.reshape(4, 8, 128)], axis=1)
    block = from_all(posterior, GROUPS[1]).reshape(32, 2, 8, 128)
    own = from_all(block, GROUPS[0]).reshape(256, 2, 8, 128)
    mine = [lax.dynamic_index_in_dim(v, slot, 0, keepdims=False) for v in (mean_new, prec_new, mom_new)]
    other = lax.ppermute(own, AXES, PARTNER)
    return (*mine, sampled(there, noise, other, sampled(here, noise, own)))


def solution(mesh):
    rows, flat = P(AXES, None), P(AXES)
    return jax.shard_map(
        on_device,
        mesh=mesh,
        in_specs=(rows, rows, rows, rows, flat, flat, flat, rows),
        out_specs=(flat, flat, flat, rows),
        check_vma=False,
    )
```

time: 127 us -> 123 us (0.969)
  blocking collectives: 73.4 us -> 87 us
  waiting for transfers between devices: 12 us -> 0.01 us
  Pallas kernels: 8.68 us -> 16.5 us
  local copies, waits for them, and re-layouts: 9.13 us -> 3.74 us
  starting transfers between devices: 17.2 us -> 12.4 us
  other arithmetic: 5.06 us -> 2.25 us
    all_to_all x4 -> x5, blocking collectives: 73.4 us -> 87 us  [exchanged(): return lax.all_to_all(x, AXES, 0, 0, axis_index_groups=groups, tiled=True)]
    all_to_all x1 -> x0, waiting for transfers between devices: 8.38 us -> none  [exchanged(): return lax.all_to_all(x, AXES, 0, 0, axis_index_groups=groups, tiled=True)]
    pallas_call x3 -> x4, Pallas kernels: 8.68 us -> 16.5 us  [the longest x2 8.07 us: sampled(): pl.pallas_call(sample_kernel, in_specs=[SMEM, SMEM, VMEM, VMEM] + [HBM] *...]
    unnamed x28 -> x22, local copies, waits for them, and re-layouts: 6.87 us -> 2.22 us
    convert_element_type x1 -> x0, other arithmetic: 4.46 us -> none  [on_device(): (mean.reshape(1, -1) + spread.reshape(1, -1) * noise.astype(jnp.float32))...]
    all_to_all x1 -> x0, starting transfers between devices: 3.64 us -> none  [exchanged(): return lax.all_to_all(x, AXES, 0, 0, axis_index_groups=groups, tiled=True)]
    ppermute x1, waiting for transfers between devices: 2.62 us -> 0.01 us  [on_device(): other = lax.ppermute(own, AXES, PARTNER)]
    add x1, other arithmetic: 0.32 us -> 1.85 us  [on_device(): sums, state = lax.optimization_barrier((keep + arrived, state))]
  transfers between devices with their start and end apart: 3 -> 2, of which waited for: 3 -> 0; matrix products, arithmetic and copies ran while one was open for 1% -> 1% of each run, Pallas kernels for 2% -> 5%
where the time goes in v2:
time: 123 us
  blocking collectives  87 us (71%)
  Pallas kernels  16.5 us (13%)
  starting transfers between devices  12.4 us (10%)
  local copies, waits for them, and re-layouts  3.74 us (3%)
  other arithmetic  2.25 us (2%)
    all_to_all x5, blocking collectives, exchanged(): return lax.all_to_all(x, AXES, 0, 0, axis_index_groups=groups, tiled=True)  87 us
    ppermute x1, starting transfers between devices, on_device(): arrived = lax.ppermute(send, AXES, PARTNER)  8.79 us
    pallas_call x2, Pallas kernels, sampled(): pl.pallas_call(sample_kernel, in_specs=[SMEM, SMEM, VMEM, VMEM] + [HBM] *...  8.07 us
    pallas_call x1, Pallas kernels, sums_to_send(): pl.pallas_call(fetching_kernel, in_specs=[SMEM] + [HBM] * 6, out_specs=VM...  5.74 us
    ppermute x1, starting transfers between devices, on_device(): other = lax.ppermute(own, AXES, PARTNER)  3.64 us
    pallas_call x1, Pallas kernels, sums_to_keep(): pl.pallas_call(held_kernel, grid_spec=pltpu.PrefetchScalarGridSpec(num_sc...  2.68 us
  transfers between devices with their start and end apart: 2, of which 0 were waited for; matrix products, arithmetic and copies ran while one was open for 1% of the time, Pallas kernels for 5%

profile of v2, /device:TPU:1, one launch (start us, length us, event | category | flops | bytes accessed | tf_op | source)
XLA Modules:
  0.0 122.8 jit_solution(8896397137937768839)
XLA Ops:
  0.6 0.0 copy-start.1
  0.6 0.0 copy-start.2
  0.7 0.0 copy-start.4
  0.7 0.0 copy-start.6
  0.7 5.7 %sums_to_send.1 = f32[256,2048]{1,0:T(8,128)} custom-call(s32[1]{0:T(128)S(6)} %sub.6.half_ref, bf16[512,1024]{1,0:T(8,128)(2,1)} %in_first.3, bf16[512,256]{1,0:T(8,128)(2,1)} %cot_first.3, bf16[512,256]{1,0:T(8,128)(2,1)} %in_third.3, bf16[512,1024]{1,0:T(8,128)(2,1)} %cot_third.3, bf16[2,512,1024]{2,1,0:T(8,128)(2,1)} %constant.47.clone.pick_first, ...), custom_call_target="tpu_custom_call" | custom-call | flops 1100000000 | bytes 5600000 | tf_op jit(solution)/shard_map/sums_to_send/pallas_call | solution.py:150
  6.4 8.8 %collective-permute-start = (f32[256,2048]{1,0:T(8,128)}, f32[256,2048]{1,0:T(8,128)}, u32[]{:S(2)}, u32[]{:S(2)}) collective-permute-start(f32[256,2048]{1,0:T(8,128)} %sums_to_send.1), channel_id=1, source_target_pairs={{0,32},{1,33},{2,34},{3,35},{4,36},{5,37},{6,38},{7,39},{8,40},{9,... | collective-permute-start | bytes 6291464 | tf_op jit(solution)/shard_map/ppermute | solution.py:247
  15.2 0.0 copy-done.1
  15.3 0.0 copy-done.2
  15.3 0.0 copy-done.4
  15.3 0.0 copy-done.6
  15.3 0.0 copy-start.3
  15.3 1.2 copy-done.3
  16.5 0.0 copy-start.5
  16.5 0.9 copy-done.5
  17.5 0.0 copy-start.8
  17.5 0.0 copy-start.9
  17.5 0.0 copy-start.10
  17.5 2.7 %sums_to_keep.1 = f32[256,2048]{1,0:T(8,128)S(1)} custom-call(s32[1]{0:T(128)} %bitcast.half_ref, bf16[512,1024]{1,0:T(8,128)(2,1)S(1)} %copy-done.2, bf16[512,256]{1,0:T(8,128)(2,1)S(1)} %copy-done.4, bf16[512,256]{1,0:T(8,128)(2,1)S(1)} %copy-done.5, bf16[512,1024]{1,0:T(8,128)(2,1)S(1)} %copy-done.3, bf16[2,512,1024]{2,1,0:T(8,128)(2,1)S(1)} %copy-done.1, ...), custom_call_target="tpu_custom_call" | custom-call | flops 1100000000 | bytes 5600000 | tf_op jit(solution)/shard_map/sums_to_keep/pallas_call | solution.py:169
  20.2 0.0 copy-done.8
  20.2 0.0 copy-done.9
  20.2 0.0 copy-done.10
  20.2 0.1 broadcast_select_fusion
  20.3 0.0 collective-permute-done
  20.3 1.9 %add.31 = f32[256,2048]{1,0:T(8,128)S(1)} add(f32[256,2048]{1,0:T(8,128)S(1)} %sums_to_keep.1, f32[256,2048]{1,0:T(8,128)} %collective-permute-done) | non-fusion elementwise | flops 524288 | bytes 6291456 | tf_op jit(solution)/shard_map/add | solution.py:251
  22.1 24.6 %all_to_all.25 = f32[8,32,2048]{2,1,0:T(8,128)S(1)} all-to-all(f32[8,32,2048]{2,1,0:T(8,128)S(1)} %bitcast.18), channel_id=1, replica_groups={{0,64,1,65,128,192,129,193},{2,66,3,67,130,194,131,195},{4,68,5,69,132,..., dimensions={0} | all-to-all | bytes 4194304 | tf_op jit(solution)/shard_map/all_to_all | solution.py:227
  46.8 0.1 reduce_sum.27
  46.9 0.1 reshape.31
  47.0 11.9 %all_to_all.26 = f32[8,4,2048]{2,1,0:T(4,128)S(1)} all-to-all(f32[8,4,2048]{2,1,0:T(4,128)S(1)} %reshape.31), channel_id=1, replica_groups={{0,2,4,6,384,386,388,390},{1,3,5,7,385,387,389,391},{8,10,12,14,392,394..., dimensions={0} | all-to-all | bytes 524288 | tf_op jit(solution)/shard_map/all_to_all | solution.py:227
  59.0 15.8 %all_to_all.27 = f32[4,4,5120]{2,1,0:T(4,128)S(1)} all-to-all(f32[4,4,5120]{2,1,0:T(4,128)S(1)} %broadcast_in_dim.44), channel_id=1, replica_groups={{0,8,16,24},{1,9,17,25},{2,10,18,26},{3,11,19,27},{4,12,20,28},{5,13,21..., dimensions={0} | all-to-all | bytes 655360 | tf_op jit(solution)/shard_map/all_to_all | solution.py:227
  74.8 0.1 reduce_sum.29
  75.0 11.4 %all_to_all.28 = f32[8,4,2,8,128]{4,3,2,1,0:T(8,128)S(1)} all-to-all(f32[8,4,2,8,128]{4,3,2,1,0:T(8,128)S(1)} %broadcast_in_dim.45), channel_id=1, replica_groups={{0,2,4,6,384,386,388,390},{1,3,5,7,385,387,389,391},{8,10,12,14,392,394..., dimensions={0} | all-to-all | bytes 524288 | tf_op jit(solution)/shard_map/all_to_all | solution.py:227
  86.5 0.2 broadcast_in_dim.47
  86.6 0.0 copy-start
  86.6 0.0 copy-start.7
  86.7 23.2 %all_to_all.29 = f32[8,32,2,8,128]{4,3,2,1,0:T(8,128)} all-to-all(f32[8,32,2,8,128]{4,3,2,1,0:T(8,128)S(1)} %broadcast_in_dim.47), channel_id=1, replica_groups={{0,64,1,65,128,192,129,193},{2,66,3,67,130,194,131,195},{4,68,5,69,132,..., dimensions={0} | all-to-all | bytes 4194304 | tf_op jit(solution)/shard_map/all_to_all | solution.py:227
  109.8 3.6 %collective-permute-start.1 = (f32[256,2,8,128]{3,2,1,0:T(8,128)}, f32[256,2,8,128]{3,2,1,0:T(8,128)}, u32[]{:S(2)}, u32[]{:S(2)}) collective-permute-start(f32[256,2,8,128]{3,2,1,0:T(8,128)} %bitcast.6.posterior), channel_id=1, source_target_pairs={{0,32},{1,33},{2,34},{3,35},{4,36},{5,37},{6,38},{7,39},{8,40},{9,... | collective-permute-start | bytes 6291464 | tf_op jit(solution)/shard_map/ppermute | solution.py:265
  113.5 0.6 constant_dynamic-slice_fusion.1
  114.1 0.6 constant_dynamic-slice_fusion
  114.7 0.0 copy-done
  114.7 0.0 copy-done.7
  114.7 4.0 %sampled.2.refs_0_ = bf16[1,524288]{1,0:T(2,128)(2,1)} custom-call(s32[1]{0:T(128)} %bitcast.half_ref, s32[2,256]{1,0:T(2,128)S(1)} %copy-done.7, bf16[1,524288]{1,0:T(2,128)(2,1)S(1)} %copy-done, f32[256,2,8,128]{3,2,1,0:T(8,128)} %bitcast.6.posterior), custom_call_target="tpu_custom_call" | custom-call | flops 524288 | bytes 4200000 | tf_op jit(solution)/shard_map/sampled/pallas_call | solution.py:213
  118.7 0.0 collective-permute-done.1.posterior
  118.8 4.0 %sampled.3 = bf16[1,524288]{1,0:T(2,128)(2,1)} custom-call(s32[1]{0:T(128)S(6)} %sub.6.half_ref, s32[2,256]{1,0:T(2,128)S(1)} %copy-done.7, bf16[1,524288]{1,0:T(2,128)(2,1)S(1)} %copy-done, f32[256,2,8,128]{3,2,1,0:T(8,128)} %collective-permute-done.1.posterior, bf16[1,524288]{1,0:T(2,128)(2,1)} %sampled.2.refs_0_), custom_call_target="tpu_custom_call", output_to_operand_aliasing={{}: (4, {})} | custom-call | flops 524288 | bytes 4200000 | tf_op jit(solution)/shard_map/sampled/pallas_call | solution.py:213
  (11 shorter events, 0.2 us)
Async XLA Ops:
  0.6 14.6 %copy-start.1 = (bf16[2,512,1024]{2,1,0:T(8,128)(2,1)S(1)}, bf16[2,512,1024]{2,1,0:T(8,128)(2,1)}, u32[]{:S(2)}) copy-start(bf16[2,512,1024]{2,1,0:T(8,128)(2,1)} %constant.47.clone.pick_first) | copy-start | bytes 6291460
  0.6 14.6 %copy-start.2 = (bf16[512,1024]{1,0:T(8,128)(2,1)S(1)}, bf16[512,1024]{1,0:T(8,128)(2,1)}, u32[]{:S(2)}) copy-start(bf16[512,1024]{1,0:T(8,128)(2,1)} %in_first.3) | copy-start | bytes 3145732
  0.7 14.6 %copy-start.4 = (bf16[512,256]{1,0:T(8,128)(2,1)S(1)}, bf16[512,256]{1,0:T(8,128)(2,1)}, u32[]{:S(2)}) copy-start(bf16[512,256]{1,0:T(8,128)(2,1)} %cot_first.3) | copy-start | bytes 786436
  0.7 14.6 %copy-start.6 = (bf16[2,128,256]{2,1,0:T(8,128)(2,1)S(1)}, bf16[2,128,256]{2,1,0:T(8,128)(2,1)}, u32[]{:S(2)}) copy-start(bf16[2,128,256]{2,1,0:T(8,128)(2,1)} %constant.48.clone.pick_third) | copy-start | bytes 393220
  6.4 13.9 %collective-permute-start = (f32[256,2048]{1,0:T(8,128)}, f32[256,2048]{1,0:T(8,128)}, u32[]{:S(2)}, u32[]{:S(2)}) collective-permute-start(f32[256,2048]{1,0:T(8,128)} %sums_to_send.1), channel_id=1, source_target_pairs={{0,32},{1,33},{2,34},{3,35},{4,36},{5,37},{6,38},{7,39},{8,40},{9,... | collective-permute-start | bytes 6291464 | tf_op jit(solution)/shard_map/ppermute | solution.py:247
  15.3 1.2 copy-start.3
  16.5 0.9 copy-start.5
  17.5 2.7 %copy-start.8 = (f32[1024]{0:T(1024)S(1)}, f32[1024]{0:T(1024)}, u32[]{:S(2)}) copy-start(f32[1024]{0:T(1024)} %param.18) | copy-start | bytes 12292
  17.5 2.7 %copy-start.9 = (f32[1024]{0:T(1024)S(1)}, f32[1024]{0:T(1024)}, u32[]{:S(2)}) copy-start(f32[1024]{0:T(1024)} %param.17) | copy-start | bytes 12292
  17.5 2.7 %copy-start.10 = (f32[1024]{0:T(1024)S(1)}, f32[1024]{0:T(1024)}, u32[]{:S(2)}) copy-start(f32[1024]{0:T(1024)} %param.16) | copy-start | bytes 12292
  86.6 28.1 %copy-start = (bf16[1,524288]{1,0:T(2,128)(2,1)S(1)}, bf16[1,524288]{1,0:T(2,128)(2,1)}, u32[]{:S(2)}) copy-start(bf16[1,524288]{1,0:T(2,128)(2,1)} %noise.3) | copy-start | bytes 3145732
  86.6 28.1 %copy-start.7 = (s32[2,256]{1,0:T(2,128)S(1)}, s32[2,256]{1,0:T(2,128)}, u32[]{:S(2)}) copy-start(s32[2,256]{1,0:T(2,128)} %constant.49.clone.table) | copy-start | bytes 6148
  109.8 8.9 %collective-permute-start.1 = (f32[256,2,8,128]{3,2,1,0:T(8,128)}, f32[256,2,8,128]{3,2,1,0:T(8,128)}, u32[]{:S(2)}, u32[]{:S(2)}) collective-permute-start(f32[256,2,8,128]{3,2,1,0:T(8,128)} %bitcast.6.posterior), channel_id=1, source_target_pairs={{0,32},{1,33},{2,34},{3,35},{4,36},{5,37},{6,38},{7,39},{8,40},{9,... | collective-permute-start | bytes 6291464 | tf_op jit(solution)/shard_map/ppermute | solution.py:265

commit v3 on v2

--- a/solution.py
+++ b/solution.py
@@ -137,7 +137,8 @@
 
 SUMS = jax.ShapeDtypeStruct((256, 2048), jnp.float32)
 COST = pl.CostEstimate(flops=1_100_000_000, bytes_accessed=5_600_000, transcendentals=0)
-PARAMS = pltpu.CompilerParams(vmem_limit_bytes=32 * 1024 * 1024)
+PARAMS = pltpu.CompilerParams(vmem_limit_bytes=16 * 1024 * 1024)
+SAMPLE_PARAMS = pltpu.CompilerParams(vmem_limit_bytes=16 * 1024 * 1024)
 SMEM = pl.BlockSpec(memory_space=pltpu.SMEM)
 VMEM = pl.BlockSpec(memory_space=pltpu.VMEM)
 HBM = pl.BlockSpec(memory_space=pltpu.HBM)
@@ -200,7 +201,7 @@
             rows[0:1, at] = row.reshape(1, SHARD).astype(jnp.bfloat16)
             return carry
 
-        lax.fori_loop(0, 32, step, 0, unroll=8)
+        lax.fori_loop(0, 32, step, 0, unroll=32)
         part = pl.ds(pl.multiple_of(first * SHARD, 32 * SHARD), 32 * SHARD)
         copies.append(pltpu.make_async_copy(rows.at[:, part], out.at[:, part], sems.at[run]))
         copies[-1].start()
@@ -217,7 +218,7 @@
         out_shape=jax.ShapeDtypeStruct(noise.shape, jnp.bfloat16),
         scratch_shapes=[pltpu.VMEM(noise.shape, jnp.bfloat16), pltpu.SemaphoreType.DMA((8,))],
         input_output_aliases={4: 0} if begun else {},
-        compiler_params=PARAMS,
+        compiler_params=SAMPLE_PARAMS,
         cost_estimate=pl.CostEstimate(flops=524288, bytes_accessed=4_200_000, transcendentals=0),
         name="sampled",
     )(half, jnp.asarray(table), noise, posterior, *begun)
@@ -246,22 +247,25 @@
     send = sums_to_send(there, *arrays)
     arrived = lax.ppermute(send, AXES, PARTNER)
     keep = sums_to_keep(here, *arrays)
-    state = jnp.concatenate([mean_old, prec_old, mom_old])
-    state = jnp.where(jnp.arange(4)[:, None] == slot, state[None], 0.0)
-    sums, state = lax.optimization_barrier((keep + arrived, state))
+    own_row = jnp.broadcast_to((jnp.arange(4)[:, None] == slot).astype(jnp.float32), (4, SHARD))
+
+    def in_own_row(v):
+        return jnp.where(own_row > 0.5, v[None], 0.0)
+
+    state = jnp.concatenate([in_own_row(0.9 * mom_old + 0.1 * mean_old), in_own_row(prec_old)], axis=1)
+    sums, state, mean_row, own_row = lax.optimization_barrier((keep + arrived, state, in_own_row(mean_old), own_row))
     sums = summed(sums.reshape(8, 32, 2048), GROUPS[0]).reshape(8, 4, 2048)
     sums = summed(sums, GROUPS[1])
-    total = from_all(jnp.concatenate([sums, state], axis=1), GROUPS[2]).sum(axis=0)
-    grad, curv, mean_4, prec_4, mom_4 = (total[:, 1024 * i : 1024 * (i + 1)] for i in range(5))
-    prec_new = 0.5 * prec_4 + 0.5 * curv
-    mom_new = 0.9 * mom_4 + grad + 0.1 * mean_4
+    total = from_all(jnp.concatenate([sums + state, mean_row], axis=1), GROUPS[2]).sum(axis=0)
+    mom_new, mean_4 = total[:, :1024], total[:, 2048:]
+    prec_new = 0.5 * total[:, 1024:2048]
     divisor = prec_new + 0.1 + 0.05
     mean_new = mean_4 - 0.3 * mom_new / divisor
     spread = jnp.sqrt(0.3 / divisor)
     posterior = jnp.stack([mean_new.reshape(4, 8, 128), spread.reshape(4, 8, 128)], axis=1)
     block = from_all(posterior, GROUPS[1]).reshape(32, 2, 8, 128)
     own = from_all(block, GROUPS[0]).reshape(256, 2, 8, 128)
-    mine = [lax.dynamic_index_in_dim(v, slot, 0, keepdims=False) for v in (mean_new, prec_new, mom_new)]
+    mine = [jnp.where(own_row > 0.5, v, 0.0).sum(axis=0) for v in (mean_new, prec_new, mom_new)]
     other = lax.ppermute(own, AXES, PARTNER)
     return (*mine, sampled(there, noise, other, sampled(here, noise, own)))
 

time: 123 us -> 119 us (0.967)
  Pallas kernels: 16.5 us -> 13.4 us
  blocking collectives: 87 us -> 84.7 us
    pallas_call x2, Pallas kernels: 8.07 us -> 5.02 us  [sampled(): pl.pallas_call(sample_kernel, in_specs=[SMEM, SMEM, VMEM, VMEM] + [HBM] *...]
    all_to_all x5, blocking collectives: 87 us -> 84.7 us  [exchanged(): return lax.all_to_all(x, AXES, 0, 0, axis_index_groups=groups, tiled=True)]
  transfers between devices with their start and end apart: 2 -> 2, of which waited for: 0 -> 1; matrix products, arithmetic and copies ran while one was open for 1% -> 0% of each run, Pallas kernels for 5% -> 4%
where the time goes in v3:
time: 119 us
  blocking collectives  84.7 us (71%)
  Pallas kernels  13.4 us (11%)
  starting transfers between devices  13.2 us (11%)
  other arithmetic  2.88 us (2%)
  local copies, waits for them, and re-layouts  2.59 us (2%)
  waiting for transfers between devices  1.23 us (1%)
    all_to_all x5, blocking collectives, exchanged(): return lax.all_to_all(x, AXES, 0, 0, axis_index_groups=groups, tiled=True)  84.7 us
    ppermute x1, starting transfers between devices, on_device(): arrived = lax.ppermute(send, AXES, PARTNER)  8.79 us
    pallas_call x1, Pallas kernels, sums_to_send(): pl.pallas_call(fetching_kernel, in_specs=[SMEM] + [HBM] * 6, out_specs=VM...  5.74 us
    pallas_call x2, Pallas kernels, sampled(): pl.pallas_call(sample_kernel, in_specs=[SMEM, SMEM, VMEM, VMEM] + [HBM] *...  5.02 us
    ppermute x1, starting transfers between devices, on_device(): other = lax.ppermute(own, AXES, PARTNER)  4.38 us
    pallas_call x1, Pallas kernels, sums_to_keep(): pl.pallas_call(held_kernel, grid_spec=pltpu.PrefetchScalarGridSpec(num_sc...  2.68 us
  transfers between devices with their start and end apart: 2, of which 1 were waited for; matrix products, arithmetic and copies ran while one was open for 0% of the time, Pallas kernels for 4%

profile of v3, /device:TPU:1, one launch (start us, length us, event | category | flops | bytes accessed | tf_op | source)
XLA Modules:
  0.0 118.9 jit_solution(10225634096491856696)
XLA Ops:
  0.6 0.0 copy-start.1
  0.6 0.0 copy-start.2
  0.7 0.0 copy-start.4
  0.7 0.0 copy-start.6
  0.7 5.7 %sums_to_send.1 = f32[256,2048]{1,0:T(8,128)} custom-call(s32[1]{0:T(128)S(6)} %sub.6.half_ref, bf16[512,1024]{1,0:T(8,128)(2,1)} %in_first.3, bf16[512,256]{1,0:T(8,128)(2,1)} %cot_first.3, bf16[512,256]{1,0:T(8,128)(2,1)} %in_third.3, bf16[512,1024]{1,0:T(8,128)(2,1)} %cot_third.3, bf16[2,512,1024]{2,1,0:T(8,128)(2,1)} %constant.39.clone.pick_first, ...), custom_call_target="tpu_custom_call" | custom-call | flops 1100000000 | bytes 5600000 | tf_op jit(solution)/shard_map/sums_to_send/pallas_call | solution.py:151
  6.4 8.8 %collective-permute-start = (f32[256,2048]{1,0:T(8,128)}, f32[256,2048]{1,0:T(8,128)}, u32[]{:S(2)}, u32[]{:S(2)}) collective-permute-start(f32[256,2048]{1,0:T(8,128)} %sums_to_send.1), channel_id=1, source_target_pairs={{0,32},{1,33},{2,34},{3,35},{4,36},{5,37},{6,38},{7,39},{8,40},{9,... | collective-permute-start | bytes 6291464 | tf_op jit(solution)/shard_map/ppermute | solution.py:248
  15.2 0.0 copy-done.1
  15.3 0.0 copy-done.2
  15.3 0.0 copy-done.4
  15.3 0.0 copy-done.6
  15.3 0.0 copy-start.3
  15.3 1.2 %copy-done.3 = bf16[512,1024]{1,0:T(8,128)(2,1)S(1)} copy-done((bf16[512,1024]{1,0:T(8,128)(2,1)S(1)}, bf16[512,1024]{1,0:T(8,128)(2,1)}, u32[]{:S(2)}) %copy-start.3) | copy-done | bytes 1048600
  16.5 0.0 copy-start.5
  16.5 0.9 copy-done.5
  17.5 0.0 copy-start.8
  17.5 0.0 copy-start.9
  17.5 0.0 copy-start.10
  17.5 2.7 %sums_to_keep.1 = f32[256,2048]{1,0:T(8,128)S(1)} custom-call(s32[1]{0:T(128)} %bitcast.half_ref, bf16[512,1024]{1,0:T(8,128)(2,1)S(1)} %copy-done.2, bf16[512,256]{1,0:T(8,128)(2,1)S(1)} %copy-done.4, bf16[512,256]{1,0:T(8,128)(2,1)S(1)} %copy-done.5, bf16[512,1024]{1,0:T(8,128)(2,1)S(1)} %copy-done.3, bf16[2,512,1024]{2,1,0:T(8,128)(2,1)S(1)} %copy-done.1, ...), custom_call_target="tpu_custom_call" | custom-call | flops 1100000000 | bytes 5600000 | tf_op jit(solution)/shard_map/sums_to_keep/pallas_call | solution.py:170
  20.2 0.0 copy-done.8
  20.2 0.0 copy-done.9
  20.2 0.0 copy-done.10
  20.2 0.1 broadcast_select_fusion
  20.3 0.0 collective-permute-done
  20.3 1.9 %add.22 = f32[256,2048]{1,0:T(8,128)S(1)} add(f32[256,2048]{1,0:T(8,128)S(1)} %sums_to_keep.1, f32[256,2048]{1,0:T(8,128)} %collective-permute-done) | non-fusion elementwise | flops 524288 | bytes 6291456 | tf_op jit(solution)/shard_map/add | solution.py:256
  22.2 0.1 broadcast_in_dim.63
  22.3 24.6 %all_to_all.25 = f32[8,32,2048]{2,1,0:T(8,128)S(1)} all-to-all(f32[8,32,2048]{2,1,0:T(8,128)S(1)} %bitcast.17), channel_id=1, replica_groups={{0,64,1,65,128,192,129,193},{2,66,3,67,130,194,131,195},{4,68,5,69,132,..., dimensions={0} | all-to-all | bytes 4194304 | tf_op jit(solution)/shard_map/all_to_all | solution.py:228
  46.9 0.1 reduce_sum.54
  47.0 0.1 reshape.35
  47.1 11.9 %all_to_all.26 = f32[8,4,2048]{2,1,0:T(4,128)S(1)} all-to-all(f32[8,4,2048]{2,1,0:T(4,128)S(1)} %reshape.35), channel_id=1, replica_groups={{0,2,4,6,384,386,388,390},{1,3,5,7,385,387,389,391},{8,10,12,14,392,394..., dimensions={0} | all-to-all | bytes 524288 | tf_op jit(solution)/shard_map/all_to_all | solution.py:228
  59.1 13.8 %all_to_all.27 = f32[4,4,3072]{2,1,0:T(4,128)S(1)} all-to-all(f32[4,4,3072]{2,1,0:T(4,128)S(1)} %broadcast_in_dim.64), channel_id=1, replica_groups={{0,8,16,24},{1,9,17,25},{2,10,18,26},{3,11,19,27},{4,12,20,28},{5,13,21..., dimensions={0} | all-to-all | bytes 393216 | tf_op jit(solution)/shard_map/all_to_all | solution.py:228
  72.9 0.6 select_reduce_fusion
  73.6 11.7 %all_to_all.28 = f32[8,4,2,8,128]{4,3,2,1,0:T(8,128)S(1)} all-to-all(f32[8,4,2,8,128]{4,3,2,1,0:T(8,128)S(1)} %broadcast_in_dim.65), channel_id=1, replica_groups={{0,2,4,6,384,386,388,390},{1,3,5,7,385,387,389,391},{8,10,12,14,392,394..., dimensions={0} | all-to-all | bytes 524288 | tf_op jit(solution)/shard_map/all_to_all | solution.py:228
  85.3 0.2 broadcast_in_dim.67
  85.5 0.0 copy-start
  85.5 0.0 copy-start.7
  85.5 22.8 %all_to_all.29 = f32[8,32,2,8,128]{4,3,2,1,0:T(8,128)S(1)} all-to-all(f32[8,32,2,8,128]{4,3,2,1,0:T(8,128)S(1)} %broadcast_in_dim.67), channel_id=1, replica_groups={{0,64,1,65,128,192,129,193},{2,66,3,67,130,194,131,195},{4,68,5,69,132,..., dimensions={0} | all-to-all | bytes 4194304 | tf_op jit(solution)/shard_map/all_to_all | solution.py:228
  108.2 4.4 %collective-permute-start.1 = (f32[256,2,8,128]{3,2,1,0:T(8,128)S(1)}, f32[256,2,8,128]{3,2,1,0:T(8,128)S(1)}, u32[]{:S(2)}, u32[]{:S(2)}) collective-permute-start(f32[256,2,8,128]{3,2,1,0:T(8,128)S(1)} %bitcast.15), channel_id=1, source_target_pairs={{0,32},{1,33},{2,34},{3,35},{4,36},{5,37},{6,38},{7,39},{8,40},{9,... | collective-permute-start | bytes 6291464 | tf_op jit(solution)/shard_map/ppermute | solution.py:269
  112.6 0.0 copy-done
  112.6 0.0 copy-done.7
  112.7 2.5 %sampled.2.refs_0_ = bf16[1,524288]{1,0:T(2,128)(2,1)} custom-call(s32[1]{0:T(128)} %bitcast.half_ref, s32[2,256]{1,0:T(2,128)S(1)} %copy-done.7, bf16[1,524288]{1,0:T(2,128)(2,1)S(1)} %copy-done, f32[256,2,8,128]{3,2,1,0:T(8,128)S(1)} %bitcast.16), custom_call_target="tpu_custom_call" | custom-call | flops 524288 | bytes 4200000 | tf_op jit(solution)/shard_map/sampled/pallas_call | solution.py:214
  115.2 1.2 %collective-permute-done.1.posterior = f32[256,2,8,128]{3,2,1,0:T(8,128)S(1)} collective-permute-done((f32[256,2,8,128]{3,2,1,0:T(8,128)S(1)}, f32[256,2,8,128]{3,2,1,0:T(8,128)S(1)}, u32[]{:S(2)}, u32[]{:S(2)}) %collective-permute-start.1) | collective-permute-done | bytes 2097184 | tf_op jit(solution)/shard_map/ppermute | solution.py:269
  116.4 2.5 %sampled.3 = bf16[1,524288]{1,0:T(2,128)(2,1)} custom-call(s32[1]{0:T(128)S(6)} %sub.6.half_ref, s32[2,256]{1,0:T(2,128)S(1)} %copy-done.7, bf16[1,524288]{1,0:T(2,128)(2,1)S(1)} %copy-done, f32[256,2,8,128]{3,2,1,0:T(8,128)S(1)} %collective-permute-done.1.posterior, bf16[1,524288]{1,0:T(2,128)(2,1)} %sampled.2.refs_0_), custom_call_target="tpu_custom_call", output_to_operand_aliasing={{}: (4, {})} | custom-call | flops 524288 | bytes 4200000 | tf_op jit(solution)/shard_map/sampled/pallas_call | solution.py:214
  (13 shorter events, 0.2 us)
Async XLA Ops:
  0.6 14.6 %copy-start.1 = (bf16[2,512,1024]{2,1,0:T(8,128)(2,1)S(1)}, bf16[2,512,1024]{2,1,0:T(8,128)(2,1)}, u32[]{:S(2)}) copy-start(bf16[2,512,1024]{2,1,0:T(8,128)(2,1)} %constant.39.clone.pick_first) | copy-start | bytes 6291460
  0.6 14.6 %copy-start.2 = (bf16[512,1024]{1,0:T(8,128)(2,1)S(1)}, bf16[512,1024]{1,0:T(8,128)(2,1)}, u32[]{:S(2)}) copy-start(bf16[512,1024]{1,0:T(8,128)(2,1)} %in_first.3) | copy-start | bytes 3145732
  0.7 14.6 %copy-start.4 = (bf16[512,256]{1,0:T(8,128)(2,1)S(1)}, bf16[512,256]{1,0:T(8,128)(2,1)}, u32[]{:S(2)}) copy-start(bf16[512,256]{1,0:T(8,128)(2,1)} %cot_first.3) | copy-start | bytes 786436
  0.7 14.6 %copy-start.6 = (bf16[2,128,256]{2,1,0:T(8,128)(2,1)S(1)}, bf16[2,128,256]{2,1,0:T(8,128)(2,1)}, u32[]{:S(2)}) copy-start(bf16[2,128,256]{2,1,0:T(8,128)(2,1)} %constant.40.clone.pick_third) | copy-start | bytes 393220
  6.4 13.9 %collective-permute-start = (f32[256,2048]{1,0:T(8,128)}, f32[256,2048]{1,0:T(8,128)}, u32[]{:S(2)}, u32[]{:S(2)}) collective-permute-start(f32[256,2048]{1,0:T(8,128)} %sums_to_send.1), channel_id=1, source_target_pairs={{0,32},{1,33},{2,34},{3,35},{4,36},{5,37},{6,38},{7,39},{8,40},{9,... | collective-permute-start | bytes 6291464 | tf_op jit(solution)/shard_map/ppermute | solution.py:248
  15.3 1.2 %copy-start.3 = (bf16[512,1024]{1,0:T(8,128)(2,1)S(1)}, bf16[512,1024]{1,0:T(8,128)(2,1)}, u32[]{:S(2)}) copy-start(bf16[512,1024]{1,0:T(8,128)(2,1)} %cot_third.3) | copy-start | bytes 3145732
  16.5 0.9 copy-start.5
  17.5 2.7 %copy-start.8 = (f32[1024]{0:T(1024)S(1)}, f32[1024]{0:T(1024)}, u32[]{:S(2)}) copy-start(f32[1024]{0:T(1024)} %param.16) | copy-start | bytes 12292
  17.5 2.7 %copy-start.9 = (f32[1024]{0:T(1024)S(1)}, f32[1024]{0:T(1024)}, u32[]{:S(2)}) copy-start(f32[1024]{0:T(1024)} %param.18) | copy-start | bytes 12292
  17.5 2.7 %copy-start.10 = (f32[1024]{0:T(1024)S(1)}, f32[1024]{0:T(1024)}, u32[]{:S(2)}) copy-start(f32[1024]{0:T(1024)} %param.17) | copy-start | bytes 12292
  85.5 27.2 %copy-start = (bf16[1,524288]{1,0:T(2,128)(2,1)S(1)}, bf16[1,524288]{1,0:T(2,128)(2,1)}, u32[]{:S(2)}) copy-start(bf16[1,524288]{1,0:T(2,128)(2,1)} %noise.3) | copy-start | bytes 3145732
  85.5 27.2 %copy-start.7 = (s32[2,256]{1,0:T(2,128)S(1)}, s32[2,256]{1,0:T(2,128)}, u32[]{:S(2)}) copy-start(s32[2,256]{1,0:T(2,128)} %constant.41.clone.table) | copy-start | bytes 6148
  108.2 8.2 %collective-permute-start.1 = (f32[256,2,8,128]{3,2,1,0:T(8,128)S(1)}, f32[256,2,8,128]{3,2,1,0:T(8,128)S(1)}, u32[]{:S(2)}, u32[]{:S(2)}) collective-permute-start(f32[256,2,8,128]{3,2,1,0:T(8,128)S(1)} %bitcast.15), channel_id=1, source_target_pairs={{0,32},{1,33},{2,34},{3,35},{4,36},{5,37},{6,38},{7,39},{8,40},{9,... | collective-permute-start | bytes 6291464 | tf_op jit(solution)/shard_map/ppermute | solution.py:269

commit v4 on v3

--- a/solution.py
+++ b/solution.py
@@ -137,7 +137,7 @@
 
 SUMS = jax.ShapeDtypeStruct((256, 2048), jnp.float32)
 COST = pl.CostEstimate(flops=1_100_000_000, bytes_accessed=5_600_000, transcendentals=0)
-PARAMS = pltpu.CompilerParams(vmem_limit_bytes=16 * 1024 * 1024)
+PARAMS = pltpu.CompilerParams(vmem_limit_bytes=48 * 1024 * 1024)
 SAMPLE_PARAMS = pltpu.CompilerParams(vmem_limit_bytes=16 * 1024 * 1024)
 SMEM = pl.BlockSpec(memory_space=pltpu.SMEM)
 VMEM = pl.BlockSpec(memory_space=pltpu.VMEM)
@@ -186,6 +186,28 @@
     )(half, *arrays)
 
 
+def add_kernel(kept, arrived, out, held, sems):
+    parts = [pl.ds(32 * i, 32) for i in range(8)]
+    copies = [pltpu.make_async_copy(arrived.at[p], held.at[p], sems.at[i]) for i, p in enumerate(parts)]
+    for copy in copies:
+        copy.start()
+    for copy, p in zip(copies, parts):
+        copy.wait()
+        out[p, :] = kept[p, :] + held[p, :]
+
+
+def added(kept, arrived):
+    return pl.pallas_call(
+        add_kernel,
+        in_specs=[VMEM, HBM],
+        out_specs=VMEM,
+        out_shape=SUMS,
+        scratch_shapes=[pltpu.VMEM((256, 2048), jnp.float32), pltpu.SemaphoreType.DMA((8,))],
+        compiler_params=SAMPLE_PARAMS,
+        name="added",
+    )(kept, arrived)
+
+
 def sample_kernel(half_ref, table, noise, posterior, *refs):
     out, rows, sems = refs[-3:]
     half = half_ref[0]
@@ -253,7 +275,7 @@
         return jnp.where(own_row > 0.5, v[None], 0.0)
 
     state = jnp.concatenate([in_own_row(0.9 * mom_old + 0.1 * mean_old), in_own_row(prec_old)], axis=1)
-    sums, state, mean_row, own_row = lax.optimization_barrier((keep + arrived, state, in_own_row(mean_old), own_row))
+    sums, state, mean_row, own_row = lax.optimization_barrier((added(keep, arrived), state, in_own_row(mean_old), own_row))
     sums = summed(sums.reshape(8, 32, 2048), GROUPS[0]).reshape(8, 4, 2048)
     sums = summed(sums, GROUPS[1])
     total = from_all(jnp.concatenate([sums + state, mean_row], axis=1), GROUPS[2]).sum(axis=0)

time: 119 us -> 118 us (level)
  Pallas kernels: 13.4 us -> 16.3 us
  local copies, waits for them, and re-layouts: 2.59 us -> 0.43 us
  other arithmetic: 2.88 us -> 0.99 us
    unnamed x22 -> x20, local copies, waits for them, and re-layouts: 2.22 us -> 0.06 us
    add x1 -> x0, other arithmetic: 1.89 us -> none  [on_device(): keep + arrived]
    pallas_call x0 -> x1, Pallas kernels: none -> 1.6 us  [added(): pl.pallas_call(add_kernel, in_specs=[VMEM, HBM], out_specs=VMEM, out_shap...]
    pallas_call x1, Pallas kernels: 2.68 us -> 3.9 us  [sums_to_keep(): pl.pallas_call(held_kernel, grid_spec=pltpu.PrefetchScalarGridSpec(num_sc...]
  transfers between devices with their start and end apart: 2 -> 2, of which waited for: 1 -> 1; matrix products, arithmetic and copies ran while one was open for 0% -> 0% of each run, Pallas kernels for 4% -> 5%
where the time goes in v4:
time: 118 us
  blocking collectives  84.8 us (72%)
  Pallas kernels  16.3 us (14%)
  starting transfers between devices  13.4 us (11%)
  waiting for transfers between devices  1.23 us (1%)
    all_to_all x5, blocking collectives, exchanged(): return lax.all_to_all(x, AXES, 0, 0, axis_index_groups=groups, tiled=True)  84.8 us
    ppermute x1, starting transfers between devices, on_device(): arrived = lax.ppermute(send, AXES, PARTNER)  8.79 us
    pallas_call x1, Pallas kernels, sums_to_send(): pl.pallas_call(fetching_kernel, in_specs=[SMEM] + [HBM] * 6, out_specs=VM...  5.74 us
    pallas_call x2, Pallas kernels, sampled(): pl.pallas_call(sample_kernel, in_specs=[SMEM, SMEM, VMEM, VMEM] + [HBM] *...  5.02 us
    ppermute x1, starting transfers between devices, on_device(): other = lax.ppermute(own, AXES, PARTNER)  4.6 us
    pallas_call x1, Pallas kernels, sums_to_keep(): pl.pallas_call(held_kernel, grid_spec=pltpu.PrefetchScalarGridSpec(num_sc...  3.9 us
  transfers between devices with their start and end apart: 2, of which 1 were waited for; matrix products, arithmetic and copies ran while one was open for 0% of the time, Pallas kernels for 5%

profile of v4, /device:TPU:1, one launch (start us, length us, event | category | flops | bytes accessed | tf_op | source)
XLA Modules:
  0.0 118.0 jit_solution(7680622197245420291)
XLA Ops:
  0.6 0.0 copy-start.1
  0.6 0.0 copy-start.2
  0.7 0.0 copy-start.3
  0.7 0.0 copy-start.4
  0.7 0.0 copy-start.5
  0.7 5.7 %sums_to_send.1 = f32[256,2048]{1,0:T(8,128)} custom-call(s32[1]{0:T(128)S(6)} %sub.6.half_ref, bf16[512,1024]{1,0:T(8,128)(2,1)} %in_first.3, bf16[512,256]{1,0:T(8,128)(2,1)} %cot_first.3, bf16[512,256]{1,0:T(8,128)(2,1)} %in_third.3, bf16[512,1024]{1,0:T(8,128)(2,1)} %cot_third.3, bf16[2,512,1024]{2,1,0:T(8,128)(2,1)} %constant.39.clone.pick_first, ...), custom_call_target="tpu_custom_call" | custom-call | flops 1100000000 | bytes 5600000 | tf_op jit(solution)/shard_map/sums_to_send/pallas_call | solution.py:151
  6.4 8.8 %collective-permute-start = (f32[256,2048]{1,0:T(8,128)}, f32[256,2048]{1,0:T(8,128)}, u32[]{:S(2)}, u32[]{:S(2)}) collective-permute-start(f32[256,2048]{1,0:T(8,128)} %sums_to_send.1), channel_id=1, source_target_pairs={{0,32},{1,33},{2,34},{3,35},{4,36},{5,37},{6,38},{7,39},{8,40},{9,... | collective-permute-start | bytes 6291464 | tf_op jit(solution)/shard_map/ppermute | solution.py:270
  15.2 0.0 copy-done.1
  15.3 0.0 copy-done.2
  15.3 0.0 copy-done.3
  15.3 0.0 copy-done.4
  15.3 0.0 copy-done.5
  15.3 0.0 copy-start.7
  15.3 0.0 copy-start.8
  15.3 0.0 copy-start.9
  15.3 3.9 %sums_to_keep.1.kept = f32[256,2048]{1,0:T(8,128)S(1)} custom-call(s32[1]{0:T(128)} %bitcast.half_ref, bf16[512,1024]{1,0:T(8,128)(2,1)S(1)} %copy-done.1, bf16[512,256]{1,0:T(8,128)(2,1)S(1)} %copy-done.3, bf16[512,256]{1,0:T(8,128)(2,1)S(1)} %copy-done.4, bf16[512,1024]{1,0:T(8,128)(2,1)S(1)} %copy-done.2, ...), custom_call_target="tpu_custom_call" | custom-call | flops 1100000000 | bytes 5600000 | tf_op jit(solution)/shard_map/sums_to_keep/pallas_call | solution.py:170
  19.3 0.0 copy-done.7
  19.3 0.0 copy-done.8
  19.3 0.0 copy-done.9
  19.3 0.1 broadcast_select_fusion
  19.4 0.0 collective-permute-done.arrived
  19.4 1.6 %added.1 = f32[256,2048]{1,0:T(8,128)S(1)} custom-call(f32[256,2048]{1,0:T(8,128)S(1)} %sums_to_keep.1.kept, f32[256,2048]{1,0:T(8,128)} %collective-permute-done.arrived), custom_call_target="tpu_custom_call" | custom-call | tf_op jit(solution)/shard_map/added/pallas_call | solution.py:200
  21.0 0.1 broadcast_in_dim.63
  21.1 24.6 %all_to_all.25 = f32[8,32,2048]{2,1,0:T(8,128)S(1)} all-to-all(f32[8,32,2048]{2,1,0:T(8,128)S(1)} %bitcast.15), channel_id=1, replica_groups={{0,64,1,65,128,192,129,193},{2,66,3,67,130,194,131,195},{4,68,5,69,132,..., dimensions={0} | all-to-all | bytes 4194304 | tf_op jit(solution)/shard_map/all_to_all | solution.py:250
  45.7 0.1 reduce_sum.54
  45.8 0.1 reshape.35
  45.9 11.9 %all_to_all.26 = f32[8,4,2048]{2,1,0:T(4,128)S(1)} all-to-all(f32[8,4,2048]{2,1,0:T(4,128)S(1)} %reshape.35), channel_id=1, replica_groups={{0,2,4,6,384,386,388,390},{1,3,5,7,385,387,389,391},{8,10,12,14,392,394..., dimensions={0} | all-to-all | bytes 524288 | tf_op jit(solution)/shard_map/all_to_all | solution.py:250
  57.9 13.8 %all_to_all.27 = f32[4,4,3072]{2,1,0:T(4,128)S(1)} all-to-all(f32[4,4,3072]{2,1,0:T(4,128)S(1)} %broadcast_in_dim.64), channel_id=1, replica_groups={{0,8,16,24},{1,9,17,25},{2,10,18,26},{3,11,19,27},{4,12,20,28},{5,13,21..., dimensions={0} | all-to-all | bytes 393216 | tf_op jit(solution)/shard_map/all_to_all | solution.py:250
  71.7 0.6 select_reduce_fusion
  72.4 11.7 %all_to_all.28 = f32[8,4,2,8,128]{4,3,2,1,0:T(8,128)S(1)} all-to-all(f32[8,4,2,8,128]{4,3,2,1,0:T(8,128)S(1)} %broadcast_in_dim.65), channel_id=1, replica_groups={{0,2,4,6,384,386,388,390},{1,3,5,7,385,387,389,391},{8,10,12,14,392,394..., dimensions={0} | all-to-all | bytes 524288 | tf_op jit(solution)/shard_map/all_to_all | solution.py:250
  84.1 0.2 broadcast_in_dim.67
  84.3 0.0 copy-start
  84.3 0.0 copy-start.6
  84.3 22.8 %all_to_all.29 = f32[8,32,2,8,128]{4,3,2,1,0:T(8,128)S(1)} all-to-all(f32[8,32,2,8,128]{4,3,2,1,0:T(8,128)S(1)} %broadcast_in_dim.67), channel_id=1, replica_groups={{0,64,1,65,128,192,129,193},{2,66,3,67,130,194,131,195},{4,68,5,69,132,..., dimensions={0} | all-to-all | bytes 4194304 | tf_op jit(solution)/shard_map/all_to_all | solution.py:250
  107.1 4.6 %collective-permute-start.1 = (f32[256,2,8,128]{3,2,1,0:T(8,128)S(1)}, f32[256,2,8,128]{3,2,1,0:T(8,128)S(1)}, u32[]{:S(2)}, u32[]{:S(2)}) collective-permute-start(f32[256,2,8,128]{3,2,1,0:T(8,128)S(1)} %bitcast.16), channel_id=1, source_target_pairs={{0,32},{1,33},{2,34},{3,35},{4,36},{5,37},{6,38},{7,39},{8,40},{9,... | collective-permute-start | bytes 6291464 | tf_op jit(solution)/shard_map/ppermute | solution.py:291
  111.7 0.0 copy-done
  111.7 0.0 copy-done.6
  111.8 2.5 %sampled.2.refs_0_ = bf16[1,524288]{1,0:T(2,128)(2,1)} custom-call(s32[1]{0:T(128)} %bitcast.half_ref, s32[2,256]{1,0:T(2,128)S(1)} %copy-done.6, bf16[1,524288]{1,0:T(2,128)(2,1)S(1)} %copy-done, f32[256,2,8,128]{3,2,1,0:T(8,128)S(1)} %bitcast.17), custom_call_target="tpu_custom_call" | custom-call | flops 524288 | bytes 4200000 | tf_op jit(solution)/shard_map/sampled/pallas_call | solution.py:236
  114.3 1.2 %collective-permute-done.1.posterior = f32[256,2,8,128]{3,2,1,0:T(8,128)S(1)} collective-permute-done((f32[256,2,8,128]{3,2,1,0:T(8,128)S(1)}, f32[256,2,8,128]{3,2,1,0:T(8,128)S(1)}, u32[]{:S(2)}, u32[]{:S(2)}) %collective-permute-start.1) | collective-permute-done | bytes 2097184 | tf_op jit(solution)/shard_map/ppermute | solution.py:291
  115.5 2.5 %sampled.3 = bf16[1,524288]{1,0:T(2,128)(2,1)} custom-call(s32[1]{0:T(128)S(6)} %sub.6.half_ref, s32[2,256]{1,0:T(2,128)S(1)} %copy-done.6, bf16[1,524288]{1,0:T(2,128)(2,1)S(1)} %copy-done, f32[256,2,8,128]{3,2,1,0:T(8,128)S(1)} %collective-permute-done.1.posterior, bf16[1,524288]{1,0:T(2,128)(2,1)} %sampled.2.refs_0_), custom_call_target="tpu_custom_call", output_to_operand_aliasing={{}: (4, {})} | custom-call | flops 524288 | bytes 4200000 | tf_op jit(solution)/shard_map/sampled/pallas_call | solution.py:236
  (13 shorter events, 0.2 us)
Async XLA Ops:
  0.6 14.6 %copy-start.1 = (bf16[512,1024]{1,0:T(8,128)(2,1)S(1)}, bf16[512,1024]{1,0:T(8,128)(2,1)}, u32[]{:S(2)}) copy-start(bf16[512,1024]{1,0:T(8,128)(2,1)} %in_first.3) | copy-start | bytes 3145732
  0.6 14.6 %copy-start.2 = (bf16[512,1024]{1,0:T(8,128)(2,1)S(1)}, bf16[512,1024]{1,0:T(8,128)(2,1)}, u32[]{:S(2)}) copy-start(bf16[512,1024]{1,0:T(8,128)(2,1)} %cot_third.3) | copy-start | bytes 3145732
  0.7 14.6 %copy-start.3 = (bf16[512,256]{1,0:T(8,128)(2,1)S(1)}, bf16[512,256]{1,0:T(8,128)(2,1)}, u32[]{:S(2)}) copy-start(bf16[512,256]{1,0:T(8,128)(2,1)} %cot_first.3) | copy-start | bytes 786436
  0.7 14.6 %copy-start.4 = (bf16[512,256]{1,0:T(8,128)(2,1)S(1)}, bf16[512,256]{1,0:T(8,128)(2,1)}, u32[]{:S(2)}) copy-start(bf16[512,256]{1,0:T(8,128)(2,1)} %in_third.3) | copy-start | bytes 786436
  0.7 14.6 %copy-start.5 = (bf16[2,128,256]{2,1,0:T(8,128)(2,1)S(1)}, bf16[2,128,256]{2,1,0:T(8,128)(2,1)}, u32[]{:S(2)}) copy-start(bf16[2,128,256]{2,1,0:T(8,128)(2,1)} %constant.40.clone.pick_third) | copy-start | bytes 393220
  6.4 13.0 %collective-permute-start = (f32[256,2048]{1,0:T(8,128)}, f32[256,2048]{1,0:T(8,128)}, u32[]{:S(2)}, u32[]{:S(2)}) collective-permute-start(f32[256,2048]{1,0:T(8,128)} %sums_to_send.1), channel_id=1, source_target_pairs={{0,32},{1,33},{2,34},{3,35},{4,36},{5,37},{6,38},{7,39},{8,40},{9,... | collective-permute-start | bytes 6291464 | tf_op jit(solution)/shard_map/ppermute | solution.py:270
  15.3 4.0 %copy-start.7 = (f32[1024]{0:T(1024)S(1)}, f32[1024]{0:T(1024)}, u32[]{:S(2)}) copy-start(f32[1024]{0:T(1024)} %param.16) | copy-start | bytes 12292
  15.3 4.0 %copy-start.8 = (f32[1024]{0:T(1024)S(1)}, f32[1024]{0:T(1024)}, u32[]{:S(2)}) copy-start(f32[1024]{0:T(1024)} %param.18) | copy-start | bytes 12292
  15.3 4.0 %copy-start.9 = (f32[1024]{0:T(1024)S(1)}, f32[1024]{0:T(1024)}, u32[]{:S(2)}) copy-start(f32[1024]{0:T(1024)} %param.17) | copy-start | bytes 12292
  84.3 27.5 %copy-start = (bf16[1,524288]{1,0:T(2,128)(2,1)S(1)}, bf16[1,524288]{1,0:T(2,128)(2,1)}, u32[]{:S(2)}) copy-start(bf16[1,524288]{1,0:T(2,128)(2,1)} %noise.3) | copy-start | bytes 3145732
  84.3 27.5 %copy-start.6 = (s32[2,256]{1,0:T(2,128)S(1)}, s32[2,256]{1,0:T(2,128)}, u32[]{:S(2)}) copy-start(s32[2,256]{1,0:T(2,128)} %constant.41.clone.table) | copy-start | bytes 6148
  107.1 8.4 %collective-permute-start.1 = (f32[256,2,8,128]{3,2,1,0:T(8,128)S(1)}, f32[256,2,8,128]{3,2,1,0:T(8,128)S(1)}, u32[]{:S(2)}, u32[]{:S(2)}) collective-permute-start(f32[256,2,8,128]{3,2,1,0:T(8,128)S(1)} %bitcast.16), channel_id=1, source_target_pairs={{0,32},{1,33},{2,34},{3,35},{4,36},{5,37},{6,38},{7,39},{8,40},{9,... | collective-permute-start | bytes 6291464 | tf_op jit(solution)/shard_map/ppermute | solution.py:291

commit v5 on v4

--- a/solution.py
+++ b/solution.py
@@ -76,7 +76,7 @@
     return lax.dot_general(a, b, (dims, ((), ())), preferred_element_type=jnp.float32)
 
 
-def half_body(half, in_first, cot_first, in_third, cot_third, pick_first, pick_third, out, ready):
+def half_body(half, in_first, cot_first, in_third, cot_third, pick_first, pick_third, out, ready, written):
     def base(b, g):
         return pl.multiple_of(jnp.where(half == 0, g * 32 + b * 16, b * 128 + g * 16), 16)
 
@@ -95,6 +95,7 @@
     grad = mm(rows.astype(jnp.bfloat16), cot_third[...])
     curv = mm(squares(rows), squares(wide))
     spread_out(1, 0, 1024, grad, curv)
+    written([base(1, g) for g in range(8)])
     ready(2)
     wide = cot_first[...].astype(jnp.float32)
     cot_sq = squares(wide)
@@ -103,10 +104,11 @@
         grad = mm(rows.astype(jnp.bfloat16), cot_first[...])
         curv = mm(squares(rows), cot_sq)
         spread_out(0, 256 * q, 256, grad, curv)
+    written([base(0, g) for g in range(8)])
 
 
 def fetching_kernel(half_ref, in_first, cot_first, in_third, cot_third, pick_first, pick_third,
-                    out, a, b, c, d, e, f, sems):
+                    out, a, b, c, d, e, f, sums, sems, out_sems):
     half = half_ref[0]
     moves = [
         ((in_third, c), (pick_third.at[half], f)),
@@ -127,12 +129,22 @@
         for copy in copies[stage]:
             copy.wait()
 
-    half_body(half, a, b, c, d, e, f, out, ready)
+    leaving = []
+
+    def written(bases):
+        for at in bases:
+            block = pl.ds(at, 16)
+            leaving.append(pltpu.make_async_copy(sums.at[block], out.at[block], out_sems.at[len(leaving)]))
+            leaving[-1].start()
+
+    half_body(half, a, b, c, d, e, f, sums, ready, written)
+    for copy in leaving:
+        copy.wait()
 
 
 def held_kernel(half_ref, in_first, cot_first, in_third, cot_third, pick_first, pick_third, out):
     half_body(half_ref[0], in_first, cot_first, in_third, cot_third, pick_first.at[0], pick_third.at[0],
-              out, lambda stage: None)
+              out, lambda stage: None, lambda bases: None)
 
 
 SUMS = jax.ShapeDtypeStruct((256, 2048), jnp.float32)
@@ -151,11 +163,12 @@
     return pl.pallas_call(
         fetching_kernel,
         in_specs=[SMEM] + [HBM] * 6,
-        out_specs=VMEM,
+        out_specs=HBM,
         out_shape=SUMS,
         scratch_shapes=[
             buffer(512, 1024), buffer(512, 256), buffer(512, 256), buffer(512, 1024),
-            buffer(512, 1024), buffer(128, 256), pltpu.SemaphoreType.DMA((6,)),
+            buffer(512, 1024), buffer(128, 256), pltpu.VMEM((256, 2048), jnp.float32),
+            pltpu.SemaphoreType.DMA((6,)), pltpu.SemaphoreType.DMA((16,)),
         ],
         compiler_params=pltpu.CompilerParams(vmem_limit_bytes=56 * 1024 * 1024),
         cost_estimate=COST,
@@ -216,14 +229,17 @@
         first = (run >> 1) * 128 + (run & 1) * 64 + half * 32
 
         def step(j, carry, run=run, first=first):
-            at = pl.ds(pl.multiple_of((first + j) * SHARD, SHARD), SHARD)
-            p = table[half, run * 32 + j]
-            normal = noise[0:1, at].astype(jnp.float32).reshape(8, 128)
-            row = posterior[p, 0] + posterior[p, 1] * normal
-            rows[0:1, at] = row.reshape(1, SHARD).astype(jnp.bfloat16)
+            at = pl.ds(pl.multiple_of((first + 4 * j) * SHARD, 4 * SHARD), 4 * SHARD)
+            normal = noise[0:1, at].astype(jnp.float32).reshape(8 * 4, 128)
+            rows_of = []
+            for k in range(4):
+                p = table[half, run * 32 + 4 * j + k]
+                rows_of.append(posterior[p, 0] + posterior[p, 1] * normal[8 * k : 8 * k + 8])
+            row = jnp.concatenate(rows_of, axis=0)
+            rows[0:1, at] = row.reshape(1, 4 * SHARD).astype(jnp.bfloat16)
             return carry
 
-        lax.fori_loop(0, 32, step, 0, unroll=32)
+        lax.fori_loop(0, 32 // 4, step, 0, unroll=32 // 4)
         part = pl.ds(pl.multiple_of(first * SHARD, 32 * SHARD), 32 * SHARD)
         copies.append(pltpu.make_async_copy(rows.at[:, part], out.at[:, part], sems.at[run]))
         copies[-1].start()

time: 118 us -> 118 us (level)
  no operation moved by 1% of the time
where the time goes in v5:
time: 118 us
  blocking collectives  84.8 us (72%)
  Pallas kernels  15.7 us (13%)
  starting transfers between devices  13.4 us (11%)
  waiting for transfers between devices  1.42 us (1%)
    all_to_all x5, blocking collectives, exchanged(): return lax.all_to_all(x, AXES, 0, 0, axis_index_groups=groups, tiled=True)  84.8 us
    ppermute x1, starting transfers between devices, on_device(): arrived = lax.ppermute(send, AXES, PARTNER)  8.78 us
    pallas_call x1, Pallas kernels, sums_to_send(): pl.pallas_call(fetching_kernel, in_specs=[SMEM] + [HBM] * 6, out_specs=HB...  5.52 us
    pallas_call x2, Pallas kernels, sampled(): pl.pallas_call(sample_kernel, in_specs=[SMEM, SMEM, VMEM, VMEM] + [HBM] *...  4.65 us
    ppermute x1, starting transfers between devices, on_device(): other = lax.ppermute(own, AXES, PARTNER)  4.6 us
    pallas_call x1, Pallas kernels, sums_to_keep(): pl.pallas_call(held_kernel, grid_spec=pltpu.PrefetchScalarGridSpec(num_sc...  3.89 us
  transfers between devices with their start and end apart: 2, of which 1 were waited for; matrix products, arithmetic and copies ran while one was open for 0% of the time, Pallas kernels for 5%

profile of v5, /device:TPU:1, one launch (start us, length us, event | category | flops | bytes accessed | tf_op | source)
XLA Modules:
  0.0 117.6 jit_solution(13931462686630115525)
XLA Ops:
  0.6 0.0 copy-start.1
  0.6 0.0 copy-start.2
  0.7 0.0 copy-start.3
  0.7 0.0 copy-start.4
  0.7 0.0 copy-start.5
  0.7 5.5 %sums_to_send.1 = f32[256,2048]{1,0:T(8,128)} custom-call(s32[1]{0:T(128)S(6)} %sub.6.half_ref, bf16[512,1024]{1,0:T(8,128)(2,1)} %in_first.3, bf16[512,256]{1,0:T(8,128)(2,1)} %cot_first.3, bf16[512,256]{1,0:T(8,128)(2,1)} %in_third.3, bf16[512,1024]{1,0:T(8,128)(2,1)} %cot_third.3, bf16[2,512,1024]{2,1,0:T(8,128)(2,1)} %constant.39.clone.pick_first, ...), custom_call_target="tpu_custom_call" | custom-call | flops 1100000000 | bytes 5600000 | tf_op jit(solution)/shard_map/sums_to_send/pallas_call | solution.py:163
  6.2 8.8 %collective-permute-start = (f32[256,2048]{1,0:T(8,128)}, f32[256,2048]{1,0:T(8,128)}, u32[]{:S(2)}, u32[]{:S(2)}) collective-permute-start(f32[256,2048]{1,0:T(8,128)} %sums_to_send.1), channel_id=1, source_target_pairs={{0,32},{1,33},{2,34},{3,35},{4,36},{5,37},{6,38},{7,39},{8,40},{9,... | collective-permute-start | bytes 6291464 | tf_op jit(solution)/shard_map/ppermute | solution.py:286
  15.0 0.0 copy-done.1
  15.0 0.0 copy-done.2
  15.0 0.0 copy-done.3
  15.0 0.0 copy-done.4
  15.1 0.0 copy-done.5
  15.1 0.0 copy-start.7
  15.1 0.0 copy-start.8
  15.1 0.0 copy-start.9
  15.1 3.9 %sums_to_keep.1.kept = f32[256,2048]{1,0:T(8,128)S(1)} custom-call(s32[1]{0:T(128)} %bitcast.half_ref, bf16[512,1024]{1,0:T(8,128)(2,1)S(1)} %copy-done.1, bf16[512,256]{1,0:T(8,128)(2,1)S(1)} %copy-done.3, bf16[512,256]{1,0:T(8,128)(2,1)S(1)} %copy-done.4, bf16[512,1024]{1,0:T(8,128)(2,1)S(1)} %copy-done.2, ...), custom_call_target="tpu_custom_call" | custom-call | flops 1100000000 | bytes 5600000 | tf_op jit(solution)/shard_map/sums_to_keep/pallas_call | solution.py:183
  19.0 0.0 copy-done.7
  19.0 0.0 copy-done.8
  19.1 0.0 copy-done.9
  19.1 0.1 broadcast_select_fusion
  19.2 0.0 collective-permute-done.arrived
  19.2 1.6 %added.1 = f32[256,2048]{1,0:T(8,128)S(1)} custom-call(f32[256,2048]{1,0:T(8,128)S(1)} %sums_to_keep.1.kept, f32[256,2048]{1,0:T(8,128)} %collective-permute-done.arrived), custom_call_target="tpu_custom_call" | custom-call | tf_op jit(solution)/shard_map/added/pallas_call | solution.py:213
  20.8 0.1 broadcast_in_dim.63
  20.9 24.6 %all_to_all.25 = f32[8,32,2048]{2,1,0:T(8,128)S(1)} all-to-all(f32[8,32,2048]{2,1,0:T(8,128)S(1)} %bitcast.15), channel_id=1, replica_groups={{0,64,1,65,128,192,129,193},{2,66,3,67,130,194,131,195},{4,68,5,69,132,..., dimensions={0} | all-to-all | bytes 4194304 | tf_op jit(solution)/shard_map/all_to_all | solution.py:266
  45.5 0.1 reduce_sum.54
  45.6 0.1 reshape.35
  45.7 11.9 %all_to_all.26 = f32[8,4,2048]{2,1,0:T(4,128)S(1)} all-to-all(f32[8,4,2048]{2,1,0:T(4,128)S(1)} %reshape.35), channel_id=1, replica_groups={{0,2,4,6,384,386,388,390},{1,3,5,7,385,387,389,391},{8,10,12,14,392,394..., dimensions={0} | all-to-all | bytes 524288 | tf_op jit(solution)/shard_map/all_to_all | solution.py:266
  57.7 13.8 %all_to_all.27 = f32[4,4,3072]{2,1,0:T(4,128)S(1)} all-to-all(f32[4,4,3072]{2,1,0:T(4,128)S(1)} %broadcast_in_dim.64), channel_id=1, replica_groups={{0,8,16,24},{1,9,17,25},{2,10,18,26},{3,11,19,27},{4,12,20,28},{5,13,21..., dimensions={0} | all-to-all | bytes 393216 | tf_op jit(solution)/shard_map/all_to_all | solution.py:266
  71.5 0.6 select_reduce_fusion
  72.2 11.7 %all_to_all.28 = f32[8,4,2,8,128]{4,3,2,1,0:T(8,128)S(1)} all-to-all(f32[8,4,2,8,128]{4,3,2,1,0:T(8,128)S(1)} %broadcast_in_dim.65), channel_id=1, replica_groups={{0,2,4,6,384,386,388,390},{1,3,5,7,385,387,389,391},{8,10,12,14,392,394..., dimensions={0} | all-to-all | bytes 524288 | tf_op jit(solution)/shard_map/all_to_all | solution.py:266
  83.9 0.2 broadcast_in_dim.67
  84.0 0.0 copy-start
  84.1 0.0 copy-start.6
  84.1 22.8 %all_to_all.29 = f32[8,32,2,8,128]{4,3,2,1,0:T(8,128)S(1)} all-to-all(f32[8,32,2,8,128]{4,3,2,1,0:T(8,128)S(1)} %broadcast_in_dim.67), channel_id=1, replica_groups={{0,64,1,65,128,192,129,193},{2,66,3,67,130,194,131,195},{4,68,5,69,132,..., dimensions={0} | all-to-all | bytes 4194304 | tf_op jit(solution)/shard_map/all_to_all | solution.py:266
  106.9 4.6 %collective-permute-start.1 = (f32[256,2,8,128]{3,2,1,0:T(8,128)S(1)}, f32[256,2,8,128]{3,2,1,0:T(8,128)S(1)}, u32[]{:S(2)}, u32[]{:S(2)}) collective-permute-start(f32[256,2,8,128]{3,2,1,0:T(8,128)S(1)} %bitcast.16), channel_id=1, source_target_pairs={{0,32},{1,33},{2,34},{3,35},{4,36},{5,37},{6,38},{7,39},{8,40},{9,... | collective-permute-start | bytes 6291464 | tf_op jit(solution)/shard_map/ppermute | solution.py:307
  111.5 0.0 copy-done
  111.5 0.0 copy-done.6
  111.5 2.3 %sampled.2.refs_0_ = bf16[1,524288]{1,0:T(2,128)(2,1)} custom-call(s32[1]{0:T(128)} %bitcast.half_ref, s32[2,256]{1,0:T(2,128)S(1)} %copy-done.6, bf16[1,524288]{1,0:T(2,128)(2,1)S(1)} %copy-done, f32[256,2,8,128]{3,2,1,0:T(8,128)S(1)} %bitcast.17), custom_call_target="tpu_custom_call" | custom-call | flops 524288 | bytes 4200000 | tf_op jit(solution)/shard_map/sampled/pallas_call | solution.py:252
  113.9 1.4 %collective-permute-done.1.posterior = f32[256,2,8,128]{3,2,1,0:T(8,128)S(1)} collective-permute-done((f32[256,2,8,128]{3,2,1,0:T(8,128)S(1)}, f32[256,2,8,128]{3,2,1,0:T(8,128)S(1)}, u32[]{:S(2)}, u32[]{:S(2)}) %collective-permute-start.1) | collective-permute-done | bytes 2097184 | tf_op jit(solution)/shard_map/ppermute | solution.py:307
  115.3 2.3 %sampled.3 = bf16[1,524288]{1,0:T(2,128)(2,1)} custom-call(s32[1]{0:T(128)S(6)} %sub.6.half_ref, s32[2,256]{1,0:T(2,128)S(1)} %copy-done.6, bf16[1,524288]{1,0:T(2,128)(2,1)S(1)} %copy-done, f32[256,2,8,128]{3,2,1,0:T(8,128)S(1)} %collective-permute-done.1.posterior, bf16[1,524288]{1,0:T(2,128)(2,1)} %sampled.2.refs_0_), custom_call_target="tpu_custom_call", output_to_operand_aliasing={{}: (4, {})} | custom-call | flops 524288 | bytes 4200000 | tf_op jit(solution)/shard_map/sampled/pallas_call | solution.py:252
  (13 shorter events, 0.2 us)
Async XLA Ops:
  0.6 14.4 %copy-start.1 = (bf16[512,1024]{1,0:T(8,128)(2,1)S(1)}, bf16[512,1024]{1,0:T(8,128)(2,1)}, u32[]{:S(2)}) copy-start(bf16[512,1024]{1,0:T(8,128)(2,1)} %in_first.3) | copy-start | bytes 3145732
  0.6 14.4 %copy-start.2 = (bf16[512,1024]{1,0:T(8,128)(2,1)S(1)}, bf16[512,1024]{1,0:T(8,128)(2,1)}, u32[]{:S(2)}) copy-start(bf16[512,1024]{1,0:T(8,128)(2,1)} %cot_third.3) | copy-start | bytes 3145732
  0.7 14.4 %copy-start.3 = (bf16[512,256]{1,0:T(8,128)(2,1)S(1)}, bf16[512,256]{1,0:T(8,128)(2,1)}, u32[]{:S(2)}) copy-start(bf16[512,256]{1,0:T(8,128)(2,1)} %cot_first.3) | copy-start | bytes 786436
  0.7 14.4 %copy-start.4 = (bf16[512,256]{1,0:T(8,128)(2,1)S(1)}, bf16[512,256]{1,0:T(8,128)(2,1)}, u32[]{:S(2)}) copy-start(bf16[512,256]{1,0:T(8,128)(2,1)} %in_third.3) | copy-start | bytes 786436
  0.7 14.4 %copy-start.5 = (bf16[2,128,256]{2,1,0:T(8,128)(2,1)S(1)}, bf16[2,128,256]{2,1,0:T(8,128)(2,1)}, u32[]{:S(2)}) copy-start(bf16[2,128,256]{2,1,0:T(8,128)(2,1)} %constant.40.clone.pick_third) | copy-start | bytes 393220
  6.2 13.0 %collective-permute-start = (f32[256,2048]{1,0:T(8,128)}, f32[256,2048]{1,0:T(8,128)}, u32[]{:S(2)}, u32[]{:S(2)}) collective-permute-start(f32[256,2048]{1,0:T(8,128)} %sums_to_send.1), channel_id=1, source_target_pairs={{0,32},{1,33},{2,34},{3,35},{4,36},{5,37},{6,38},{7,39},{8,40},{9,... | collective-permute-start | bytes 6291464 | tf_op jit(solution)/shard_map/ppermute | solution.py:286
  15.1 4.0 %copy-start.7 = (f32[1024]{0:T(1024)S(1)}, f32[1024]{0:T(1024)}, u32[]{:S(2)}) copy-start(f32[1024]{0:T(1024)} %param.16) | copy-start | bytes 12292
  15.1 4.0 %copy-start.8 = (f32[1024]{0:T(1024)S(1)}, f32[1024]{0:T(1024)}, u32[]{:S(2)}) copy-start(f32[1024]{0:T(1024)} %param.18) | copy-start | bytes 12292
  15.1 4.0 %copy-start.9 = (f32[1024]{0:T(1024)S(1)}, f32[1024]{0:T(1024)}, u32[]{:S(2)}) copy-start(f32[1024]{0:T(1024)} %param.17) | copy-start | bytes 12292
  84.0 27.5 %copy-start = (bf16[1,524288]{1,0:T(2,128)(2,1)S(1)}, bf16[1,524288]{1,0:T(2,128)(2,1)}, u32[]{:S(2)}) copy-start(bf16[1,524288]{1,0:T(2,128)(2,1)} %noise.3) | copy-start | bytes 3145732
  84.1 27.5 %copy-start.6 = (s32[2,256]{1,0:T(2,128)S(1)}, s32[2,256]{1,0:T(2,128)}, u32[]{:S(2)}) copy-start(s32[2,256]{1,0:T(2,128)} %constant.41.clone.table) | copy-start | bytes 6148
  106.9 8.4 %collective-permute-start.1 = (f32[256,2,8,128]{3,2,1,0:T(8,128)S(1)}, f32[256,2,8,128]{3,2,1,0:T(8,128)S(1)}, u32[]{:S(2)}, u32[]{:S(2)}) collective-permute-start(f32[256,2,8,128]{3,2,1,0:T(8,128)S(1)} %bitcast.16), channel_id=1, source_target_pairs={{0,32},{1,33},{2,34},{3,35},{4,36},{5,37},{6,38},{7,39},{8,40},{9,... | collective-permute-start | bytes 6291464 | tf_op jit(solution)/shard_map/ppermute | solution.py:307
